TPU v7x, 256 devices: a whole 4x4x8 slice. The times are simulated.
256 devices in a mesh: section: 2 (over core), expert: 32 (over y, z), mp: 4 (over x).
Axes of the slice: x: 4, y: 4, z: 8, core: 2. Of those that a mesh axis runs over, the one named last changes fastest.
Arguments:
- layer_inputs: bfloat16 [2, 8192, 2048], P('section', ('expert', 'mp')), may hold values from -6 to 6
- norm_gain: float32 [2, 2048], P('section'), may hold values from 0.1 to 1.9
- w_gate: bfloat16 [2, 64, 768, 2048], P('section', 'expert', 'mp'), may hold values from -0.125 to 0.125
- w_up: bfloat16 [2, 64, 768, 2048], P('section', 'expert', 'mp'), may hold values from -0.125 to 0.125
- w_down: bfloat16 [2, 64, 768, 2048], P('section', 'expert', 'mp'), may hold values from -0.21875 to 0.21875
- routes: int32 [2, 8192, 8], P('section', ('expert', 'mp')), may hold values from 0 to 63, all different within a row; in each aligned block of 32 rows (0 to 31, 32 to 63, ..., all dimensions but the last counted through in order) at most 5 rows name the same one
- probs: float32 [2, 8192, 8], P('section', ('expert', 'mp')), may hold values from 0.05 to 0.3
- cotangent: bfloat16 [8192, 2048], P(('expert', 'mp')), may hold values from -6 to 6
- sampled: int32 [1], replicated, may hold values from 0 to 1
Outputs:
- input_grads: bfloat16 [2, 8192, 2048], P('section', ('expert', 'mp'))
- gate_grads: float32 [2, 64, 768, 2048], P('section', 'expert', 'mp')
- up_grads: float32 [2, 64, 768, 2048], P('section', 'expert', 'mp')
Inputs may be any that keep to these rules, and one draw needn't show every extreme that they name: `routes`: each row names 8 different experts and every expert is named somewhere. In each aligned block of 32 rows of a layer, no expert is named by more than 5 rows, and in some blocks one expert is named by exactly 5.
All inputs are finite; a program needn't handle non-finite values.
Results may differ from a plain program's by a relative error of at most 0.012.
Values may be sent and summed in bfloat16 or wider, within the bound.
No kernel may reach another device: no remote copies, remote signals or barrier semaphores. Data moves between devices by JAX's collectives and lax.ppermute only.
A program may use at most 192 MiB of HBM per device.

v0:
```python
import functools

import jax
import jax.numpy as jnp
from jax import lax
from jax.experimental import pallas as pl
from jax.experimental.pallas import tpu as pltpu
from jax.sharding import PartitionSpec as P


CAPH = 5
CAP = 2 * CAPH
LANES = 128


epsilon = 1e-06


def other_core(value):
    return lax.ppermute(value, "section", [(0, 1), (1, 0)])


def after(value, *earlier):
    return lax.optimization_barrier((value, *earlier))[0]


def turned(value, by):
    peers = lax.axis_size("mp")
    return lax.ppermute(value, "mp", [(i, (i + by) % peers) for i in range(peers)])


def ring_first(own):
    return turned(own, 1), turned(own, -1)


def ring_second(before, behind):
    half = before.shape[-2] // 2
    return (
        turned(before[..., :half, :], 1),
        turned(behind[..., half:, :], -1),
    )


def pick_kernel(index_ref, gate_ref, up_ref, down_ref, out_ref):
    out_ref[0] = gate_ref[0]
    out_ref[1] = up_ref[0]
    out_ref[2] = down_ref[0]


def expert_part(index, weights, blocks):
    _, units, width = weights[0].shape
    rows = units // blocks
    spec = pl.BlockSpec((1, rows, width), lambda i, index_ref: (index_ref[0], i, 0))
    return pl.pallas_call(
        pick_kernel,
        grid_spec=pltpu.PrefetchScalarGridSpec(
            num_scalar_prefetch=1,
            grid=(blocks,),
            in_specs=[spec] * 3,
            out_specs=pl.BlockSpec((3, rows, width), lambda i, index_ref: (0, i, 0)),
        ),
        out_shape=jax.ShapeDtypeStruct((3, units, width), weights[0].dtype),
        name="expert_part",
    )(index, *weights)


def choose_kernel(keep, index_ref, got_ref, gate_ref, up_ref, down_ref, out_ref):
    @pl.when(index_ref[0] == keep)
    def _():
        out_ref[0] = gate_ref[0]
        out_ref[1] = up_ref[0]
        out_ref[2] = down_ref[0]

    @pl.when(index_ref[0] != keep)
    def _():
        out_ref[...] = got_ref[...]


def layer_part(layer, first, count, blocks, index, got, weights):
    _, units, width = weights[0].shape
    rows = units // blocks
    own = pl.BlockSpec((1, rows, width), lambda i, index_ref: (index_ref[0], first + i, 0))
    return pl.pallas_call(
        functools.partial(choose_kernel, layer),
        grid_spec=pltpu.PrefetchScalarGridSpec(
            num_scalar_prefetch=1,
            grid=(count,),
            in_specs=[pl.BlockSpec((3, rows, width), lambda i, index_ref: (0, first + i, 0))]
            + [own] * 3,
            out_specs=pl.BlockSpec((3, rows, width), lambda i, index_ref: (0, i, 0)),
        ),
        out_shape=jax.ShapeDtypeStruct((3, count * rows, width), weights[0].dtype),
        name="layer_part",
    )(index, got, *weights)


def normalize(inputs, gain_vector):
    values = inputs.astype(jnp.float32)
    factor = lax.rsqrt(jnp.mean(values * values, axis=1, keepdims=True) + epsilon)
    normed = values * factor
    return (normed, factor, (normed * gain_vector[None, :]).astype(jnp.bfloat16))


def plan(token_routes, token_probs, experts_here):
    match = token_routes[:, :, None] == experts_here[None, None, :]
    named = jnp.any(match, axis=1)
    chance = jnp.sum(jnp.where(match, token_probs[:, :, None], 0.0), axis=1)
    tokens = token_routes.shape[0]
    earlier = (
        jnp.arange(tokens, dtype=jnp.int32)[:, None] > jnp.arange(tokens, dtype=jnp.int32)[None, :]
    )
    places = jnp.dot(
        earlier.astype(jnp.bfloat16),
        named.astype(jnp.bfloat16),
        preferred_element_type=jnp.float32,
    ).astype(jnp.int32)
    places = jnp.where(named, places, -1).T
    pick = places[:, None, :] == jnp.arange(CAP, dtype=jnp.int32)[None, :, None]
    row_prob = jnp.sum(jnp.where(pick, chance.T[:, None, :], 0.0), axis=2)
    return pick, row_prob


def to_wire(rows, peers):
    return rows.reshape(peers, rows.shape[0] // peers, rows.shape[1] // LANES, LANES)


def from_wire(wire):
    return wire.reshape(wire.shape[0] * wire.shape[1], wire.shape[2] * wire.shape[3])


def exchange(rows, peers):
    wire = to_wire(rows, peers)
    return from_wire(lax.all_to_all(wire, "expert", split_axis=0, concat_axis=0, tiled=True))


def back_rows(weights, rows):
    return lax.dot_general(
        weights, rows, (((0,), (0,)), ((), ())), preferred_element_type=jnp.float32
    )


def expert_kernel(pieces, hidden_ref, weighted_ref, *refs):
    weight_refs, (slot_ref, d_ref, held, sems) = refs[:pieces], refs[pieces:]
    parts, _, units, width = held.shape
    rows = weight_refs[0].shape[1]
    each = units // rows

    def place(part, number):
        return held.at[part, :, pl.ds(number * rows, rows), :]

    for number, ref in enumerate(weight_refs):
        part = number // each
        pltpu.make_async_copy(ref, place(part, number % each), sems.at[number]).start()

    def along(rows_ref, part, which):
        return lax.dot_general(
            rows_ref[...],
            held[part, which],
            (((1,), (1,)), ((), ())),
            preferred_element_type=jnp.float32,
        )

    def one_part(part, carry):
        for number in range(each):
            there = place(part, number)
            pltpu.make_async_copy(there, there, sems.at[part * each + number]).wait()
        gate_act = along(hidden_ref, part, 0)
        lifted = along(hidden_ref, part, 1)
        back = along(weighted_ref, part, 2)
        logistic = jax.nn.sigmoid(gate_act)
        d_gate = back * lifted * logistic * (1.0 + gate_act * (1.0 - logistic))
        d_up = back * gate_act * logistic
        d_ref[part] = jnp.concatenate([d_gate, d_up], axis=1).astype(jnp.bfloat16)
        return carry

    lax.fori_loop(0, parts, one_part, 0)
    step = min(256, width)

    def one_column(number, carry):
        columns = pl.ds(pl.multiple_of(number * step, step), step)
        total = None
        for part in range(parts):
            both = held[part, 0:2, :, columns].reshape(2 * units, step)
            term = jnp.dot(d_ref[part], both, preferred_element_type=jnp.float32)
            total = term if total is None else total + term
        slot_ref[:, columns] = total.astype(jnp.bfloat16)
        return carry

    lax.fori_loop(0, width // step, one_column, 0)


def expert_pass(hidden_rows, weighted_rows, pieces, parts):
    count, width = hidden_rows.shape
    units = sum(piece.shape[1] for piece in pieces) // parts
    vmem = pl.BlockSpec(memory_space=pltpu.VMEM)
    return pl.pallas_call(
        functools.partial(expert_kernel, len(pieces)),
        in_specs=[vmem] * 2 + [pl.BlockSpec(memory_space=pl.ANY)] * len(pieces),
        out_specs=(vmem, vmem),
        out_shape=(
            jax.ShapeDtypeStruct((count, width), jnp.bfloat16),
            jax.ShapeDtypeStruct((parts, count, 2 * units), jnp.bfloat16),
        ),
        scratch_shapes=[
            pltpu.VMEM((parts, 3, units, width), jnp.bfloat16),
            pltpu.SemaphoreType.DMA((len(pieces),)),
        ],
        cost_estimate=pl.CostEstimate(
            flops=10 * count * width * units * parts,
            bytes_accessed=2 * width * (3 * units * parts + 3 * count),
            transcendentals=count * units * parts,
        ),
        name="expert_pass",
    )(hidden_rows, weighted_rows, *pieces)


def per_device(layer_inputs, norm_gain, w_gate, w_up, w_down, routes, probs, cotangent, sampled):
    section = lax.axis_index("section")
    upper = section == 1
    peers = lax.axis_size("expert")
    groups = lax.axis_size("mp")
    tokens, width = cotangent.shape
    top_count = routes.shape[2]

    stored = (w_gate[0], w_up[0], w_down[0])
    index = section.astype(jnp.int32).reshape(1)
    got = other_core(expert_part(1 - index, stored, 4))
    head1 = layer_part(1, 0, 2, 4, index, got, stored)
    tail1 = layer_part(1, 2, 2, 4, index, got, stored)
    head_before = turned(head1, 1)
    tail_behind = turned(tail1, -1)
    tail_before = turned(tail1, 1)
    head_behind = turned(head1, -1)
    head_far = turned(head_before, 1)
    tail_far = turned(tail_behind, -1)
    small = jnp.concatenate(
        [norm_gain[0], routes[0].astype(jnp.float32).reshape(-1), probs[0].reshape(-1)]
    )
    small_parts = lax.all_gather(small, "section", axis=0)
    input_parts = lax.all_gather(layer_inputs[0], "section", axis=0)
    own0 = layer_part(0, 0, 4, 4, index, after(got, tail1), stored)
    before0, behind0 = ring_first(after(own0, head_far, tail_far))
    far0 = turned(before0, 1)
    pieces1 = (
        head1,
        tail1,
        head_before,
        tail_before,
        head_behind,
        tail_behind,
        head_far,
        tail_far,
    )
    pieces0 = (own0, before0, behind0, far0)

    experts_here = 2 * jnp.arange(peers, dtype=jnp.int32) + section
    layers = []
    for layer in range(2):
        vector = small_parts[layer]
        gain_vector = vector[:width]
        token_routes = (
            vector[width : width + tokens * top_count].reshape(tokens, top_count).astype(jnp.int32)
        )
        token_probs = vector[width + tokens * top_count :].reshape(tokens, top_count)
        normed, factor, hidden = normalize(input_parts[layer], gain_vector)
        pick, row_prob = plan(token_routes, token_probs, experts_here)
        layers.append((gain_vector, normed, factor, hidden, pick, row_prob))

    def spread(pick, rows):
        flat = pick.astype(jnp.bfloat16).reshape(-1, pick.shape[2])
        return jnp.dot(flat, rows, preferred_element_type=jnp.float32)

    pick1, pick0 = layers[1][4], layers[0][4]

    def scaled_rows(pick, row_prob, upstream):
        rows = spread(pick, upstream) * row_prob.reshape(-1, 1)
        return rows.astype(jnp.bfloat16)

    first = jnp.concatenate(
        [
            to_wire(spread(pick1, layers[1][3]).astype(jnp.bfloat16), peers),
            to_wire(scaled_rows(pick1, layers[1][5], cotangent), peers),
        ],
        axis=1,
    )
    arrived = lax.all_to_all(first, "expert", split_axis=0, concat_axis=0, tiled=True)
    hidden1 = from_wire(arrived[:, :CAP])
    weighted1 = from_wire(arrived[:, CAP:])
    second = to_wire(spread(pick0, layers[0][3]).astype(jnp.bfloat16), peers)
    hidden0 = from_wire(lax.all_to_all(second, "expert", split_axis=0, concat_axis=0, tiled=True))
    trained1 = sampled[0] == 1

    def finish(layer, sent, upstream):
        gain_vector, normed, factor, _, pick, _ = layers[layer]
        returned = from_wire(
            lax.all_to_all(sent, "expert", split_axis=0, concat_axis=0, tiled=True)
        )
        flat = pick.astype(jnp.bfloat16).reshape(-1, tokens)
        partial = lax.dot_general(
            flat, returned, (((0,), (0,)), ((), ())), preferred_element_type=jnp.float32
        )
        token_grad = partial + other_core(partial)
        scaled = token_grad * gain_vector[None, :]
        inner = jnp.mean(scaled * normed, axis=1, keepdims=True)
        return (upstream.astype(jnp.float32) + factor * (scaled - normed * inner)).astype(
            jnp.bfloat16
        )

    slot_grad1, d_both1 = expert_pass(hidden1, weighted1, pieces1, groups)
    trained_hidden = jnp.where(trained1, *after((hidden1, hidden0), slot_grad1))
    before_h, behind_h = ring_first(after(trained_hidden, far0))
    far_h = ring_second(before_h, behind_h)
    far_h = jnp.concatenate(far_h, axis=0)
    input_grad1 = finish(1, to_wire(slot_grad1, peers), cotangent)
    weighted0 = exchange(scaled_rows(pick0, layers[0][5], input_grad1), peers)
    slot_grad0, d_both0 = expert_pass(hidden0, weighted0, pieces0, groups)
    sent0 = to_wire(slot_grad0, peers)
    input_grad0 = finish(0, sent0, input_grad1)
    result = jnp.where(upper, input_grad1, input_grad0)

    units = w_gate.shape[2]
    d_both = after(jnp.where(trained1, d_both1, d_both0), sent0)
    d_behind = turned(d_both[1], -1)
    d_before = turned(d_both[2], 1)
    d_far = turned(d_both[3], 2)
    grads = back_rows(d_both[0], trained_hidden)
    grads = grads + back_rows(d_before, before_h)
    grads = grads + back_rows(d_behind, behind_h)
    grads = grads + back_rows(d_far, far_h)
    grads = grads.astype(jnp.bfloat16)
    from_other = other_core(grads)
    trained = sampled[0] == section

    def on_owner(mine, theirs):
        low = jnp.where(upper, theirs, mine)
        high = jnp.where(upper, mine, theirs)
        pair = jnp.stack([low, high]).astype(jnp.float32)
        return jnp.where(trained, pair, 0.0)[None]

    gate_share = on_owner(grads[:units], from_other[:units])
    up_share = on_owner(grads[units:], from_other[units:])
    return (result[None], gate_share, up_share)


def solution(mesh):
    placed = (
        P("section", ("expert", "mp"), None),
        P("section", None),
        P("section", "expert", "mp", None),
        P("section", "expert", "mp", None),
        P("section", "expert", "mp", None),
        P("section", ("expert", "mp"), None),
        P("section", ("expert", "mp"), None),
        P(("expert", "mp"), None),
        P(),
    )
    return jax.shard_map(
        per_device,
        mesh=mesh,
        in_specs=placed,
        out_specs=(
            P("section", ("expert", "mp"), None),
            P("section", "expert", "mp", None),
            P("section", "expert", "mp", None),
        ),
        check_vma=False,
    )
```

profile of v0, /device:TPU:1, one launch (start us, length us, event | category | flops | bytes accessed | tf_op | source)
XLA Modules:
  0.0 374.4 jit_solution(289235000997789659)
XLA Ops:
  3.2 4.7 %all-gather = f32[6144]{0:T(1024)S(1)} all-gather(f32[3072]{0:T(1024)S(1)} %pad_maximum_fusion.1), channel_id=2, replica_groups=mesh['section'=2,'expert'=32,'mp'=4] {'section'}, dimensions={0}, use_global_device_ids=true | all-gather | bytes 36864 | tf_op jit(solution)/shard_map/all_gather | solution.py:239
  15.3 9.6 %all-to-all-start = ((bf16[32,20,16,128]{3,2,1,0:T(8,128)(2,1)}), bf16[32,20,16,128]{3,2,1,0:T(8,128)(2,1)}, u32[]{:S(2)}, u32[]{:S(2)}) async-start(bf16[32,20,16,128]{3,2,1,0:T(8,128)(2,1)} %pad_maximum_fusion), calls=%async_computation | async-start | bytes 5242880 | tf_op jit(solution)/shard_map/all_to_all | solution.py:286
  24.9 3.9 %expert_part.1 = bf16[3,192,2048]{2,1,0:T(8,128)(2,1)} custom-call(s32[1]{0:T(128)S(6)} %sub.9.index_ref, bf16[2,192,2048]{2,1,0:T(8,128)(2,1)} %bitcast.153, bf16[2,192,2048]{2,1,0:T(8,128)(2,1)} %bitcast.157, bf16[2,192,2048]{2,1,0:T(8,128)(2,1)} %bitcast.161), custom_call_target="tpu_custom_call" | custom-call | tf_op jit(solution)/shard_map/expert_part/pallas_call | solution.py:54
  29.5 4.4 %collective-permute-done.got_ref = bf16[3,192,2048]{2,1,0:T(8,128)(2,1)S(1)} collective-permute-done((bf16[3,192,2048]{2,1,0:T(8,128)(2,1)}, bf16[3,192,2048]{2,1,0:T(8,128)(2,1)S(1)}, u32[]{:S(2)}, u32[]{:S(2)}) %collective-permute-start) | collective-permute-done | bytes 2359328 | tf_op jit(solution)/shard_map/ppermute | solution.py:20
  35.3 2.5 layer_part.3.refs_0_
  39.0 2.5 layer_part.4.refs_1_
  44.5 22.0 %collective-permute-done.1.refs_2_ = bf16[3,96,2048]{2,1,0:T(8,128)(2,1)S(1)} collective-permute-done((bf16[3,96,2048]{2,1,0:T(8,128)(2,1)}, bf16[3,96,2048]{2,1,0:T(8,128)(2,1)S(1)}, u32[]{:S(2)}, u32[]{:S(2)}) %collective-permute-start.1) | collective-permute-done | bytes 1179680 | tf_op jit(solution)/shard_map/ppermute | solution.py:29
  68.6 2.9 collective-permute-start.6
  71.5 13.2 %all-to-all-done = bf16[32,20,16,128]{3,2,1,0:T(8,128)(2,1)} async-done(((bf16[32,20,16,128]{3,2,1,0:T(8,128)(2,1)}), bf16[32,20,16,128]{3,2,1,0:T(8,128)(2,1)}, u32[]{:S(2)}, u32[]{:S(2)}) %all-to-all-start) | async-done | bytes 2621472 | tf_op jit(solution)/shard_map/all_to_all | solution.py:286
  89.0 4.9 %collective-permute-done.3.refs_4_ = bf16[3,96,2048]{2,1,0:T(8,128)(2,1)} collective-permute-done((bf16[3,96,2048]{2,1,0:T(8,128)(2,1)S(1)}, bf16[3,96,2048]{2,1,0:T(8,128)(2,1)}, u32[]{:S(2)}, u32[]{:S(2)}) %collective-permute-start.3) | collective-permute-done | bytes 1179680 | tf_op jit(solution)/shard_map/ppermute | solution.py:29
  93.9 23.1 %collective-permute-done.5.refs_6_ = bf16[3,96,2048]{2,1,0:T(8,128)(2,1)} collective-permute-done((bf16[3,96,2048]{2,1,0:T(8,128)(2,1)S(1)}, bf16[3,96,2048]{2,1,0:T(8,128)(2,1)}, u32[]{:S(2)}, u32[]{:S(2)}) %collective-permute-start.5) | collective-permute-done | bytes 1179680 | tf_op jit(solution)/shard_map/ppermute | solution.py:29
  119.2 13.7 %expert_pass.2 = (bf16[320,2048]{1,0:T(8,128)(2,1)}, bf16[4,320,384]{2,1,0:T(8,128)(2,1)}) custom-call(bf16[320,2048]{1,0:T(8,128)(2,1)} %get-tuple-element.20.hidden_ref, bf16[320,2048]{1,0:T(8,128)(2,1)} %get-tuple-element.44.weighted_ref, bf16[3,96,2048]{2,1,0:T(8,128)(2,1)} %layer_part.3.refs_0_, bf16[3,96,2048]{2,1,0:T(8,128)(2,1)} %layer_part.4.refs_1_, ...), custom_call_target="tpu_custom_call" | custom-call | flops 5033164800 | bytes 13369344 | tf_op jit(solution)/shard_map/expert_pass/pallas_call | solution.py:196
  134.5 40.5 %all_to_all.25 = bf16[32,10,16,128]{3,2,1,0:T(8,128)(2,1)S(1)} all-to-all(bf16[32,10,16,128]{3,2,1,0:T(8,128)(2,1)S(1)} %bitcast.175), channel_id=1, replica_groups=mesh['section'=2,'expert'=32,'mp'=4] {'expert'}, dimensions={0} | all-to-all | bytes 2621440 | tf_op jit(solution)/shard_map/all_to_all | solution.py:296
  175.4 4.9 %collective-permute-start.7 = (f32[64,2048]{1,0:T(8,128)S(1)}, f32[64,2048]{1,0:T(8,128)S(1)}, u32[]{:S(2)}, u32[]{:S(2)}) collective-permute-start(f32[64,2048]{1,0:T(8,128)S(1)} %fusion.9), channel_id=1, source_target_pairs={{0,128},{128,0},{1,129},{129,1},{2,130},{130,2},{3,131},{131,3},{4... | collective-permute-start | bytes 1572872 | tf_op jit(solution)/shard_map/ppermute | solution.py:20
  184.1 4.0 %all-to-all-start.2 = ((bf16[32,10,16,128]{3,2,1,0:T(8,128)(2,1)}), bf16[32,10,16,128]{3,2,1,0:T(8,128)(2,1)S(1)}, u32[]{:S(2)}, u32[]{:S(2)}) async-start(bf16[32,10,16,128]{3,2,1,0:T(8,128)(2,1)} %bitcast.45), calls=%async_computation.2 | async-start | bytes 2621440 | tf_op jit(solution)/shard_map/all_to_all | solution.py:290
  188.1 4.3 %layer_part.5.refs_0_ = bf16[3,192,2048]{2,1,0:T(8,128)(2,1)} custom-call(s32[1]{0:T(128)} %bitcast.6.index_ref, bf16[3,192,2048]{2,1,0:T(8,128)(2,1)} %copy-done, bf16[2,192,2048]{2,1,0:T(8,128)(2,1)} %bitcast.156, bf16[2,192,2048]{2,1,0:T(8,128)(2,1)} %bitcast.160, bf16[2,192,2048]{2,1,0:T(8,128)(2,1)} %bitcast.164), custom_call_target="tpu_custom_call" | custom-call | tf_op jit(solution)/shard_map/layer_part/pallas_call | solution.py:83
  197.4 22.4 %all-to-all-done.2 = bf16[32,10,16,128]{3,2,1,0:T(8,128)(2,1)S(1)} async-done(((bf16[32,10,16,128]{3,2,1,0:T(8,128)(2,1)}), bf16[32,10,16,128]{3,2,1,0:T(8,128)(2,1)S(1)}, u32[]{:S(2)}, u32[]{:S(2)}) %all-to-all-start.2) | async-done | bytes 1310752 | tf_op jit(solution)/shard_map/all_to_all | solution.py:290
  219.8 7.1 %all-to-all-start.3 = ((bf16[32,10,16,128]{3,2,1,0:T(8,128)(2,1)}), bf16[32,10,16,128]{3,2,1,0:T(8,128)(2,1)S(1)}, u32[]{:S(2)}, u32[]{:S(2)}) async-start(bf16[32,10,16,128]{3,2,1,0:T(8,128)(2,1)} %bitcast.51), calls=%async_computation.3 | async-start | bytes 2621440 | tf_op jit(solution)/shard_map/all_to_all | solution.py:133
  226.9 19.6 %collective-permute-done.8.refs_1_ = bf16[3,192,2048]{2,1,0:T(8,128)(2,1)} collective-permute-done((bf16[3,192,2048]{2,1,0:T(8,128)(2,1)}, bf16[3,192,2048]{2,1,0:T(8,128)(2,1)}, u32[]{:S(2)}, u32[]{:S(2)}) %collective-permute-start.8) | collective-permute-done | bytes 2359328 | tf_op jit(solution)/shard_map/ppermute | solution.py:29
  246.5 2.7 collective-permute-start.9
  251.3 48.2 %collective-permute-done.10.refs_3_ = bf16[3,192,2048]{2,1,0:T(8,128)(2,1)} collective-permute-done((bf16[3,192,2048]{2,1,0:T(8,128)(2,1)}, bf16[3,192,2048]{2,1,0:T(8,128)(2,1)}, u32[]{:S(2)}, u32[]{:S(2)}) %collective-permute-start.10) | collective-permute-done | bytes 2359328 | tf_op jit(solution)/shard_map/ppermute | solution.py:29
  302.4 13.7 %expert_pass.3 = (bf16[320,2048]{1,0:T(8,128)(2,1)}, bf16[4,320,384]{2,1,0:T(8,128)(2,1)}) custom-call(bf16[320,2048]{1,0:T(8,128)(2,1)} %bitcast.173, bf16[320,2048]{1,0:T(8,128)(2,1)} %bitcast.177, bf16[3,192,2048]{2,1,0:T(8,128)(2,1)} %layer_part.5.refs_0_, bf16[3,192,2048]{2,1,0:T(8,128)(2,1)} %collective-permute-done.8.refs_1_, ...), custom_call_target="tpu_custom_call" | custom-call | flops 5033164800 | bytes 13369344 | tf_op jit(solution)/shard_map/expert_pass/pallas_call | solution.py:196
  316.1 2.7 copy.32
  318.8 8.7 %all-to-all-start.4 = ((bf16[32,10,16,128]{3,2,1,0:T(8,128)(2,1)}), bf16[32,10,16,128]{3,2,1,0:T(8,128)(2,1)S(1)}, u32[]{:S(2)}, u32[]{:S(2)}) async-start(bf16[32,10,16,128]{3,2,1,0:T(8,128)(2,1)} %bitcast.57), calls=%async_computation.4 | async-start | bytes 2621440 | tf_op jit(solution)/shard_map/all_to_all | solution.py:296
  329.0 2.4 collective-permute-start.14
  333.5 2.8 collective-permute-start.18
  337.5 3.2 collective-permute-done.12
  340.7 2.3 fusion.70
  343.0 2.3 fusion.71
  345.3 8.7 %collective-permute-done.18 = bf16[160,2048]{1,0:T(8,128)(2,1)S(1)} collective-permute-done((bf16[160,2048]{1,0:T(8,128)(2,1)S(1)}, bf16[160,2048]{1,0:T(8,128)(2,1)S(1)}, u32[]{:S(2)}, u32[]{:S(2)}) %collective-permute-start.18) | collective-permute-done | bytes 655392 | tf_op jit(solution)/shard_map/ppermute | solution.py:29
  356.6 2.7 collective-permute-start.19
  360.6 3.1 collective-permute-start.11
  (120 shorter events, 59.4 us)
Async XLA Ops:
  0.6 8.9 %copy-start.8 = (bf16[1,64,2048]{2,1,0:T(8,128)(2,1)S(1)}, bf16[1,64,2048]{2,1,0:T(8,128)(2,1)}, u32[]{:S(2)}) copy-start(bf16[1,64,2048]{2,1,0:T(8,128)(2,1)} %param.9) | copy-start | bytes 786436
  2.4 9.4 %copy-start.6 = (bf16[64,2048]{1,0:T(8,128)(2,1)S(1)}, bf16[64,2048]{1,0:T(8,128)(2,1)}, u32[]{:S(2)}) copy-start(bf16[64,2048]{1,0:T(8,128)(2,1)} %param.16) | copy-start | bytes 786436
  15.3 69.4 %all-to-all-start = ((bf16[32,20,16,128]{3,2,1,0:T(8,128)(2,1)}), bf16[32,20,16,128]{3,2,1,0:T(8,128)(2,1)}, u32[]{:S(2)}, u32[]{:S(2)}) async-start(bf16[32,20,16,128]{3,2,1,0:T(8,128)(2,1)} %pad_maximum_fusion), calls=%async_computation | async-start | bytes 5242880 | tf_op jit(solution)/shard_map/all_to_all | solution.py:286
  28.9 5.0 %collective-permute-start = (bf16[3,192,2048]{2,1,0:T(8,128)(2,1)}, bf16[3,192,2048]{2,1,0:T(8,128)(2,1)S(1)}, u32[]{:S(2)}, u32[]{:S(2)}) collective-permute-start(bf16[3,192,2048]{2,1,0:T(8,128)(2,1)} %expert_part.1), channel_id=1, source_target_pairs={{0,128},{128,0},{1,129},{129,1},{2,130},{130,2},{3,131},{131,3},{4... | collective-permute-start | bytes 7077896 | tf_op jit(solution)/shard_map/ppermute | solution.py:20
  33.9 1.4 copy-start
  37.7 5.2 %copy-start.5 = (bf16[3,96,2048]{2,1,0:T(8,128)(2,1)S(1)}, bf16[3,96,2048]{2,1,0:T(8,128)(2,1)}, u32[]{:S(2)}) copy-start(bf16[3,96,2048]{2,1,0:T(8,128)(2,1)} %layer_part.3.refs_0_) | copy-start | bytes 3538948
  37.7 28.7 %collective-permute-start.1 = (bf16[3,96,2048]{2,1,0:T(8,128)(2,1)}, bf16[3,96,2048]{2,1,0:T(8,128)(2,1)S(1)}, u32[]{:S(2)}, u32[]{:S(2)}) collective-permute-start(bf16[3,96,2048]{2,1,0:T(8,128)(2,1)} %layer_part.3.refs_0_), channel_id=1, source_target_pairs={{0,1},{1,2},{2,3},{3,0},{4,5},{5,6},{6,7},{7,4},{8,9},{9,10},{10,1... | collective-permute-start | bytes 3538952 | tf_op jit(solution)/shard_map/ppermute | solution.py:29
  41.4 27.2 %collective-permute-start.4 = (bf16[3,96,2048]{2,1,0:T(8,128)(2,1)}, bf16[3,96,2048]{2,1,0:T(8,128)(2,1)}, u32[]{:S(2)}, u32[]{:S(2)}) collective-permute-start(bf16[3,96,2048]{2,1,0:T(8,128)(2,1)} %layer_part.4.refs_1_), channel_id=1, source_target_pairs={{0,3},{1,0},{2,1},{3,2},{4,7},{5,4},{6,5},{7,6},{8,11},{9,8},{10,9... | collective-permute-start | bytes 3538952 | tf_op jit(solution)/shard_map/ppermute | solution.py:29
  43.0 50.9 %collective-permute-start.3 = (bf16[3,96,2048]{2,1,0:T(8,128)(2,1)S(1)}, bf16[3,96,2048]{2,1,0:T(8,128)(2,1)}, u32[]{:S(2)}, u32[]{:S(2)}) collective-permute-start(bf16[3,96,2048]{2,1,0:T(8,128)(2,1)S(1)} %copy-done.5), channel_id=1, source_target_pairs={{0,3},{1,0},{2,1},{3,2},{4,7},{5,4},{6,5},{7,6},{8,11},{9,8},{10,9... | collective-permute-start | bytes 3538952 | tf_op jit(solution)/shard_map/ppermute | solution.py:29
  44.2 49.8 %collective-permute-start.2 = (bf16[3,96,2048]{2,1,0:T(8,128)(2,1)}, bf16[3,96,2048]{2,1,0:T(8,128)(2,1)}, u32[]{:S(2)}, u32[]{:S(2)}) collective-permute-start(bf16[3,96,2048]{2,1,0:T(8,128)(2,1)} %layer_part.4.refs_1_), channel_id=1, source_target_pairs={{0,1},{1,2},{2,3},{3,0},{4,5},{5,6},{6,7},{7,4},{8,9},{9,10},{10,1... | collective-permute-start | bytes 3538952 | tf_op jit(solution)/shard_map/ppermute | solution.py:29
  66.4 20.4 %copy-start.9 = (bf16[3,96,2048]{2,1,0:T(8,128)(2,1)}, bf16[3,96,2048]{2,1,0:T(8,128)(2,1)S(1)}, u32[]{:S(2)}) copy-start(bf16[3,96,2048]{2,1,0:T(8,128)(2,1)S(1)} %collective-permute-done.1.refs_2_) | copy-start | bytes 3538948
  66.4 50.6 %collective-permute-start.5 = (bf16[3,96,2048]{2,1,0:T(8,128)(2,1)S(1)}, bf16[3,96,2048]{2,1,0:T(8,128)(2,1)}, u32[]{:S(2)}, u32[]{:S(2)}) collective-permute-start(bf16[3,96,2048]{2,1,0:T(8,128)(2,1)S(1)} %collective-permute-done.1.refs_2_), channel_id=1, source_target_pairs={{0,1},{1,2},{2,3},{3,0},{4,5},{5,6},{6,7},{7,4},{8,9},{9,10},{10,1... | collective-permute-start | bytes 3538952 | tf_op jit(solution)/shard_map/ppermute | solution.py:29
  68.6 50.6 %collective-permute-start.6 = (bf16[3,96,2048]{2,1,0:T(8,128)(2,1)}, bf16[3,96,2048]{2,1,0:T(8,128)(2,1)}, u32[]{:S(2)}, u32[]{:S(2)}) collective-permute-start(bf16[3,96,2048]{2,1,0:T(8,128)(2,1)} %collective-permute-done.4.refs_5_), channel_id=1, source_target_pairs={{0,3},{1,0},{2,1},{3,2},{4,7},{5,4},{6,5},{7,6},{8,11},{9,8},{10,9... | collective-permute-start | bytes 3538952 | tf_op jit(solution)/shard_map/ppermute | solution.py:29
  175.4 6.4 %collective-permute-start.7 = (f32[64,2048]{1,0:T(8,128)S(1)}, f32[64,2048]{1,0:T(8,128)S(1)}, u32[]{:S(2)}, u32[]{:S(2)}) collective-permute-start(f32[64,2048]{1,0:T(8,128)S(1)} %fusion.9), channel_id=1, source_target_pairs={{0,128},{128,0},{1,129},{129,1},{2,130},{130,2},{3,131},{131,3},{4... | collective-permute-start | bytes 1572872 | tf_op jit(solution)/shard_map/ppermute | solution.py:20
  184.1 35.6 %all-to-all-start.2 = ((bf16[32,10,16,128]{3,2,1,0:T(8,128)(2,1)}), bf16[32,10,16,128]{3,2,1,0:T(8,128)(2,1)S(1)}, u32[]{:S(2)}, u32[]{:S(2)}) async-start(bf16[32,10,16,128]{3,2,1,0:T(8,128)(2,1)} %bitcast.45), calls=%async_computation.2 | async-start | bytes 2621440 | tf_op jit(solution)/shard_map/all_to_all | solution.py:290
  192.3 54.1 %collective-permute-start.8 = (bf16[3,192,2048]{2,1,0:T(8,128)(2,1)}, bf16[3,192,2048]{2,1,0:T(8,128)(2,1)}, u32[]{:S(2)}, u32[]{:S(2)}) collective-permute-start(bf16[3,192,2048]{2,1,0:T(8,128)(2,1)} %layer_part.5.refs_0_), channel_id=1, source_target_pairs={{0,1},{1,2},{2,3},{3,0},{4,5},{5,6},{6,7},{7,4},{8,9},{9,10},{10,1... | collective-permute-start | bytes 7077896 | tf_op jit(solution)/shard_map/ppermute | solution.py:29
  219.8 81.2 %all-to-all-start.3 = ((bf16[32,10,16,128]{3,2,1,0:T(8,128)(2,1)}), bf16[32,10,16,128]{3,2,1,0:T(8,128)(2,1)S(1)}, u32[]{:S(2)}, u32[]{:S(2)}) async-start(bf16[32,10,16,128]{3,2,1,0:T(8,128)(2,1)} %bitcast.51), calls=%async_computation.3 | async-start | bytes 2621440 | tf_op jit(solution)/shard_map/all_to_all | solution.py:133
  246.5 53.0 %collective-permute-start.10 = (bf16[3,192,2048]{2,1,0:T(8,128)(2,1)}, bf16[3,192,2048]{2,1,0:T(8,128)(2,1)}, u32[]{:S(2)}, u32[]{:S(2)}) collective-permute-start(bf16[3,192,2048]{2,1,0:T(8,128)(2,1)} %collective-permute-done.8.refs_1_), channel_id=1, source_target_pairs={{0,1},{1,2},{2,3},{3,0},{4,5},{5,6},{6,7},{7,4},{8,9},{9,10},{10,1... | collective-permute-start | bytes 7077896 | tf_op jit(solution)/shard_map/ppermute | solution.py:29
  246.5 56.0 %collective-permute-start.9 = (bf16[3,192,2048]{2,1,0:T(8,128)(2,1)}, bf16[3,192,2048]{2,1,0:T(8,128)(2,1)}, u32[]{:S(2)}, u32[]{:S(2)}) collective-permute-start(bf16[3,192,2048]{2,1,0:T(8,128)(2,1)} %layer_part.5.refs_0_), channel_id=1, source_target_pairs={{0,3},{1,0},{2,1},{3,2},{4,7},{5,4},{6,5},{7,6},{8,11},{9,8},{10,9... | collective-permute-start | bytes 7077896 | tf_op jit(solution)/shard_map/ppermute | solution.py:29
  249.8 1.4 copy-start.1
  250.2 1.1 copy-start.2
  299.5 32.8 %collective-permute-start.15 = (bf16[320,2048]{1,0:T(8,128)(2,1)S(1)}, bf16[320,2048]{1,0:T(8,128)(2,1)}, u32[]{:S(2)}, u32[]{:S(2)}) collective-permute-start(bf16[320,2048]{1,0:T(8,128)(2,1)S(1)} %broadcast_select_fusion), channel_id=1, source_target_pairs={{0,3},{1,0},{2,1},{3,2},{4,7},{5,4},{6,5},{7,6},{8,11},{9,8},{10,9... | collective-permute-start | bytes 3932168 | tf_op jit(solution)/shard_map/ppermute | solution.py:29
  299.5 36.7 %collective-permute-start.13 = (bf16[320,2048]{1,0:T(8,128)(2,1)S(1)}, bf16[320,2048]{1,0:T(8,128)(2,1)}, u32[]{:S(2)}, u32[]{:S(2)}) collective-permute-start(bf16[320,2048]{1,0:T(8,128)(2,1)S(1)} %broadcast_select_fusion), channel_id=1, source_target_pairs={{0,1},{1,2},{2,3},{3,0},{4,5},{5,6},{6,7},{7,4},{8,9},{9,10},{10,1... | collective-permute-start | bytes 3932168 | tf_op jit(solution)/shard_map/ppermute | solution.py:29
  318.8 40.6 %all-to-all-start.4 = ((bf16[32,10,16,128]{3,2,1,0:T(8,128)(2,1)}), bf16[32,10,16,128]{3,2,1,0:T(8,128)(2,1)S(1)}, u32[]{:S(2)}, u32[]{:S(2)}) async-start(bf16[32,10,16,128]{3,2,1,0:T(8,128)(2,1)} %bitcast.57), calls=%async_computation.4 | async-start | bytes 2621440 | tf_op jit(solution)/shard_map/all_to_all | solution.py:296
  328.9 16.5 %collective-permute-start.16 = (bf16[320,384]{1,0:T(8,128)(2,1)S(1)}, bf16[320,384]{1,0:T(8,128)(2,1)S(1)}, u32[]{:S(2)}, u32[]{:S(2)}) collective-permute-start(bf16[320,384]{1,0:T(8,128)(2,1)S(1)} %get-tuple-element.39), channel_id=1, source_target_pairs={{0,2},{1,3},{2,0},{3,1},{4,6},{5,7},{6,4},{7,5},{8,10},{9,11},{10,... | collective-permute-start | bytes 737288 | tf_op jit(solution)/shard_map/ppermute | solution.py:29
  329.0 14.0 %collective-permute-start.14 = (bf16[320,384]{1,0:T(8,128)(2,1)S(1)}, bf16[320,384]{1,0:T(8,128)(2,1)S(1)}, u32[]{:S(2)}, u32[]{:S(2)}) collective-permute-start(bf16[320,384]{1,0:T(8,128)(2,1)S(1)} %get-tuple-element.40), channel_id=1, source_target_pairs={{0,3},{1,0},{2,1},{3,2},{4,7},{5,4},{6,5},{7,6},{8,11},{9,8},{10,9... | collective-permute-start | bytes 737288 | tf_op jit(solution)/shard_map/ppermute | solution.py:29
  331.3 9.3 %collective-permute-start.12 = (bf16[320,384]{1,0:T(8,128)(2,1)S(1)}, bf16[320,384]{1,0:T(8,128)(2,1)S(1)}, u32[]{:S(2)}, u32[]{:S(2)}) collective-permute-start(bf16[320,384]{1,0:T(8,128)(2,1)S(1)} %get-tuple-element.41), channel_id=1, source_target_pairs={{0,1},{1,2},{2,3},{3,0},{4,5},{5,6},{6,7},{7,4},{8,9},{9,10},{10,1... | collective-permute-start | bytes 737288 | tf_op jit(solution)/shard_map/ppermute | solution.py:29
  333.5 20.5 %collective-permute-start.18 = (bf16[160,2048]{1,0:T(8,128)(2,1)S(1)}, bf16[160,2048]{1,0:T(8,128)(2,1)S(1)}, u32[]{:S(2)}, u32[]{:S(2)}) collective-permute-start(bf16[160,2048]{1,0:T(8,128)(2,1)S(1)} %slice.105), channel_id=1, source_target_pairs={{0,3},{1,0},{2,1},{3,2},{4,7},{5,4},{6,5},{7,6},{8,11},{9,8},{10,9... | collective-permute-start | bytes 1966088 | tf_op jit(solution)/shard_map/ppermute | solution.py:29
  337.4 18.1 %collective-permute-start.17 = (bf16[160,2048]{1,0:T(8,128)(2,1)S(1)}, bf16[160,2048]{1,0:T(8,128)(2,1)S(1)}, u32[]{:S(2)}, u32[]{:S(2)}) collective-permute-start(bf16[160,2048]{1,0:T(8,128)(2,1)S(1)} %slice.104), channel_id=1, source_target_pairs={{0,1},{1,2},{2,3},{3,0},{4,5},{5,6},{6,7},{7,4},{8,9},{9,10},{10,1... | collective-permute-start | bytes 1966088 | tf_op jit(solution)/shard_map/ppermute | solution.py:29
  356.6 12.2 %collective-permute-start.19 = (bf16[384,2048]{1,0:T(8,128)(2,1)S(1)}, bf16[384,2048]{1,0:T(8,128)(2,1)}, u32[]{:S(2)}, u32[]{:S(2)}) collective-permute-start(bf16[384,2048]{1,0:T(8,128)(2,1)S(1)} %add_convert_fusion), channel_id=1, source_target_pairs={{0,128},{128,0},{1,129},{129,1},{2,130},{130,2},{3,131},{131,3},{4... | collective-permute-start | bytes 4718600 | tf_op jit(solution)/shard_map/ppermute | solution.py:20
  360.6 6.2 %copy-start.4 = (bf16[64,2048]{1,0:T(8,128)(2,1)S(1)}, bf16[64,2048]{1,0:T(8,128)(2,1)}, u32[]{:S(2)}) copy-start(bf16[64,2048]{1,0:T(8,128)(2,1)} %copy-done.3) | copy-start | bytes 786436
  360.6 4.9 %collective-permute-start.11 = (f32[64,2048]{1,0:T(8,128)}, f32[64,2048]{1,0:T(8,128)S(1)}, u32[]{:S(2)}, u32[]{:S(2)}) collective-permute-start(f32[64,2048]{1,0:T(8,128)} %fusion.6), channel_id=1, source_target_pairs={{0,128},{128,0},{1,129},{129,1},{2,130},{130,2},{3,131},{131,3},{4... | collective-permute-start | bytes 1572872 | tf_op jit(solution)/shard_map/ppermute | solution.py:20
  (2 other events, 1.6 us)
where the time goes:
time: 376 us; the launch traced here: 374 us
  waiting for transfers between devices  178 us (47%)
  starting transfers between devices  58.5 us (16%)
  blocking collectives  47.3 us (13%)
  Pallas kernels  40.5 us (11%)
  local copies, waits for them, and re-layouts  22.1 us (6%)
  other arithmetic  14.9 us (4%)
  matrix products  10.9 us (3%)
    ppermute x16, waiting for transfers between devices, turned(): lax.ppermute(value, 'mp', [(i, (i + by) % peers) for i in range(peers)])  135 us
    all_to_all x1, blocking collectives, finish(): lax.all_to_all(sent, 'expert', split_axis=0, concat_axis=0, tiled=True)  40.5 us
    pallas_call x2, Pallas kernels, expert_pass(): pl.pallas_call(functools.partial(expert_kernel, len(pieces)), in_specs=[v...  27.3 us
    all_to_all x1, waiting for transfers between devices, per_device(): lax.all_to_all(second, 'expert', split_axis=0, concat_axis=0, tiled=True)  22.4 us
    ppermute x16, starting transfers between devices, turned(): lax.ppermute(value, 'mp', [(i, (i + by) % peers) for i in range(peers)])  17.8 us
    unnamed x29, local copies, waits for them, and re-layouts  13.3 us
    all_to_all x1, waiting for transfers between devices, per_device(): lax.all_to_all(first, 'expert', split_axis=0, concat_axis=0, tiled=True)  13.2 us
    ppermute x4, starting transfers between devices, other_core(): return lax.ppermute(value, 'section', [(0, 1), (1, 0)])  11.4 us
  transfers between devices with their start and end apart: 24, of which 15 were waited for; matrix products, arithmetic and copies ran while one was open for 7% of the time, Pallas kernels for 7%

commit v1 on v0

--- a/solution.py
+++ b/solution.py
@@ -142,15 +142,13 @@
 def expert_kernel(pieces, hidden_ref, weighted_ref, *refs):
     weight_refs, (slot_ref, d_ref, held, sems) = refs[:pieces], refs[pieces:]
     parts, _, units, width = held.shape
-    rows = weight_refs[0].shape[1]
-    each = units // rows
-
-    def place(part, number):
-        return held.at[part, :, pl.ds(number * rows, rows), :]
-
-    for number, ref in enumerate(weight_refs):
-        part = number // each
-        pltpu.make_async_copy(ref, place(part, number % each), sems.at[number]).start()
+    start = 0
+    for ref in weight_refs:
+        rows = ref.shape[1]
+        part, first = start // units, start % units
+        there = held.at[part, :, pl.ds(first, rows), :]
+        pltpu.make_async_copy(ref, there, sems.at[part]).start()
+        start += rows
 
     def along(rows_ref, part, which):
         return lax.dot_general(
@@ -161,9 +159,7 @@
         )
 
     def one_part(part, carry):
-        for number in range(each):
-            there = place(part, number)
-            pltpu.make_async_copy(there, there, sems.at[part * each + number]).wait()
+        pltpu.make_async_copy(held.at[part], held.at[part], sems.at[part]).wait()
         gate_act = along(hidden_ref, part, 0)
         lifted = along(hidden_ref, part, 1)
         back = along(weighted_ref, part, 2)
@@ -203,7 +199,7 @@
         ),
         scratch_shapes=[
             pltpu.VMEM((parts, 3, units, width), jnp.bfloat16),
-            pltpu.SemaphoreType.DMA((len(pieces),)),
+            pltpu.SemaphoreType.DMA((parts,)),
         ],
         cost_estimate=pl.CostEstimate(
             flops=10 * count * width * units * parts,
@@ -240,7 +236,7 @@
     input_parts = lax.all_gather(layer_inputs[0], "section", axis=0)
     own0 = layer_part(0, 0, 4, 4, index, after(got, tail1), stored)
     before0, behind0 = ring_first(after(own0, head_far, tail_far))
-    far0 = turned(before0, 1)
+    far0 = ring_second(before0, behind0)
     pieces1 = (
         head1,
         tail1,
@@ -251,7 +247,7 @@
         head_far,
         tail_far,
     )
-    pieces0 = (own0, before0, behind0, far0)
+    pieces0 = (own0, before0, behind0, *far0)
 
     experts_here = 2 * jnp.arange(peers, dtype=jnp.int32) + section
     layers = []
@@ -280,14 +276,13 @@
         [
             to_wire(spread(pick1, layers[1][3]).astype(jnp.bfloat16), peers),
             to_wire(scaled_rows(pick1, layers[1][5], cotangent), peers),
+            to_wire(spread(pick0, layers[0][3]).astype(jnp.bfloat16), peers),
         ],
         axis=1,
     )
     arrived = lax.all_to_all(first, "expert", split_axis=0, concat_axis=0, tiled=True)
     hidden1 = from_wire(arrived[:, :CAP])
-    weighted1 = from_wire(arrived[:, CAP:])
-    second = to_wire(spread(pick0, layers[0][3]).astype(jnp.bfloat16), peers)
-    hidden0 = from_wire(lax.all_to_all(second, "expert", split_axis=0, concat_axis=0, tiled=True))
+    weighted1 = from_wire(arrived[:, CAP : 2 * CAP])
     trained1 = sampled[0] == 1
 
     def finish(layer, sent, upstream):
@@ -307,8 +302,9 @@
         )
 
     slot_grad1, d_both1 = expert_pass(hidden1, weighted1, pieces1, groups)
+    hidden0 = from_wire(after(arrived, slot_grad1)[:, 2 * CAP :])
     trained_hidden = jnp.where(trained1, *after((hidden1, hidden0), slot_grad1))
-    before_h, behind_h = ring_first(after(trained_hidden, far0))
+    before_h, behind_h = ring_first(after(trained_hidden, *far0))
     far_h = ring_second(before_h, behind_h)
     far_h = jnp.concatenate(far_h, axis=0)
     input_grad1 = finish(1, to_wire(slot_grad1, peers), cotangent)

time: 376 us -> 339 us (0.902)
  blocking collectives: 47.3 us -> 6.83 us
  starting transfers between devices: 58.5 us -> 75.1 us
  waiting for transfers between devices: 178 us -> 162 us
  local copies, waits for them, and re-layouts: 22.1 us -> 26.9 us
    ppermute x16 -> x17, waiting for transfers between devices: 135 us -> 87 us  [turned(): lax.ppermute(value, 'mp', [(i, (i + by) % peers) for i in range(peers)])]
    all_to_all x1 -> x0, blocking collectives: 40.5 us -> none  [finish(): lax.all_to_all(sent, 'expert', split_axis=0, concat_axis=0, tiled=True)]
    all_to_all x1, waiting for transfers between devices: 13.2 us -> 41.6 us  [per_device(): lax.all_to_all(first, 'expert', split_axis=0, concat_axis=0, tiled=True)]
    all_to_all x1 -> x2, waiting for transfers between devices: 0.01 us -> 24.2 us  [finish(): lax.all_to_all(sent, 'expert', split_axis=0, concat_axis=0, tiled=True)]
    all_to_all x1 -> x0, waiting for transfers between devices: 22.4 us -> none  [per_device(): lax.all_to_all(second, 'expert', split_axis=0, concat_axis=0, tiled=True)]
    all_to_all x1 -> x2, starting transfers between devices: 8.66 us -> 18.1 us  [finish(): lax.all_to_all(sent, 'expert', split_axis=0, concat_axis=0, tiled=True)]
    ppermute x4, starting transfers between devices: 11.4 us -> 19.7 us  [other_core(): return lax.ppermute(value, 'section', [(0, 1), (1, 0)])]
    ppermute x16 -> x17, starting transfers between devices: 17.8 us -> 22.9 us  [turned(): lax.ppermute(value, 'mp', [(i, (i + by) % peers) for i in range(peers)])]
  transfers between devices with their start and end apart: 24 -> 25, of which waited for: 15 -> 15; matrix products, arithmetic and copies ran while one was open for 7% -> 10% of each run, Pallas kernels for 7% -> 8%
where the time goes in v1:
time: 339 us; the launch traced here: 337 us
  waiting for transfers between devices  162 us (48%)
  starting transfers between devices  75.1 us (22%)
  Pallas kernels  40.4 us (12%)
  local copies, waits for them, and re-layouts  26.9 us (8%)
  other arithmetic  14.6 us (4%)
  matrix products  10.2 us (3%)
  blocking collectives  6.83 us (2%)
    ppermute x17, waiting for transfers between devices, turned(): lax.ppermute(value, 'mp', [(i, (i + by) % peers) for i in range(peers)])  87 us
    all_to_all x1, waiting for transfers between devices, per_device(): lax.all_to_all(first, 'expert', split_axis=0, concat_axis=0, tiled=True)  41.6 us
    pallas_call x2, Pallas kernels, expert_pass(): pl.pallas_call(functools.partial(expert_kernel, len(pieces)), in_specs=[v...  27.2 us
    all_to_all x2, waiting for transfers between devices, finish(): lax.all_to_all(sent, 'expert', split_axis=0, concat_axis=0, tiled=True)  24.2 us
    ppermute x17, starting transfers between devices, turned(): lax.ppermute(value, 'mp', [(i, (i + by) % peers) for i in range(peers)])  22.9 us
    ppermute x4, starting transfers between devices, other_core(): return lax.ppermute(value, 'section', [(0, 1), (1, 0)])  19.7 us
    all_to_all x2, starting transfers between devices, finish(): lax.all_to_all(sent, 'expert', split_axis=0, concat_axis=0, tiled=True)  18.1 us
    unnamed x43, local copies, waits for them, and re-layouts  16 us
  transfers between devices with their start and end apart: 25, of which 15 were waited for; matrix products, arithmetic and copies ran while one was open for 10% of the time, Pallas kernels for 8%

profile of v1, /device:TPU:1, one launch (start us, length us, event | category | flops | bytes accessed | tf_op | source)
XLA Modules:
  0.0 337.4 jit_solution(4104878346294273593)
XLA Ops:
  3.1 4.7 %all-gather = f32[6144]{0:T(1024)S(1)} all-gather(f32[3072]{0:T(1024)S(1)} %pad_maximum_fusion.1), channel_id=2, replica_groups=mesh['section'=2,'expert'=32,'mp'=4] {'section'}, dimensions={0}, use_global_device_ids=true | all-gather | bytes 36864 | tf_op jit(solution)/shard_map/all_gather | solution.py:235
  17.4 9.6 %all-to-all-start = ((bf16[32,30,16,128]{3,2,1,0:T(8,128)(2,1)}), bf16[32,30,16,128]{3,2,1,0:T(8,128)(2,1)}, u32[]{:S(2)}, u32[]{:S(2)}) async-start(bf16[32,30,16,128]{3,2,1,0:T(8,128)(2,1)} %pad_maximum_fusion), calls=%async_computation | async-start | bytes 7864320 | tf_op jit(solution)/shard_map/all_to_all | solution.py:283
  27.1 3.9 %expert_part.1 = bf16[3,192,2048]{2,1,0:T(8,128)(2,1)} custom-call(s32[1]{0:T(128)S(6)} %sub.9.index_ref, bf16[2,192,2048]{2,1,0:T(8,128)(2,1)} %bitcast.155, bf16[2,192,2048]{2,1,0:T(8,128)(2,1)} %bitcast.159, bf16[2,192,2048]{2,1,0:T(8,128)(2,1)} %bitcast.163), custom_call_target="tpu_custom_call" | custom-call | tf_op jit(solution)/shard_map/expert_part/pallas_call | solution.py:54
  31.6 4.4 %collective-permute-done.got_ref = bf16[3,192,2048]{2,1,0:T(8,128)(2,1)S(1)} collective-permute-done((bf16[3,192,2048]{2,1,0:T(8,128)(2,1)}, bf16[3,192,2048]{2,1,0:T(8,128)(2,1)S(1)}, u32[]{:S(2)}, u32[]{:S(2)}) %collective-permute-start) | collective-permute-done | bytes 2359328 | tf_op jit(solution)/shard_map/ppermute | solution.py:20
  42.4 2.5 layer_part.3.refs_0_
  47.6 20.0 %collective-permute-done.4.refs_5_ = bf16[3,96,2048]{2,1,0:T(8,128)(2,1)S(1)} collective-permute-done((bf16[3,96,2048]{2,1,0:T(8,128)(2,1)}, bf16[3,96,2048]{2,1,0:T(8,128)(2,1)S(1)}, u32[]{:S(2)}, u32[]{:S(2)}) %collective-permute-start.4) | collective-permute-done | bytes 1179680 | tf_op jit(solution)/shard_map/ppermute | solution.py:29
  67.6 3.4 %collective-permute-start.6 = (bf16[3,96,2048]{2,1,0:T(8,128)(2,1)S(1)}, bf16[3,96,2048]{2,1,0:T(8,128)(2,1)}, u32[]{:S(2)}, u32[]{:S(2)}) collective-permute-start(bf16[3,96,2048]{2,1,0:T(8,128)(2,1)S(1)} %collective-permute-done.4.refs_5_), channel_id=1, source_target_pairs={{0,3},{1,0},{2,1},{3,2},{4,7},{5,4},{6,5},{7,6},{8,11},{9,8},{10,9... | collective-permute-start | bytes 3538952 | tf_op jit(solution)/shard_map/ppermute | solution.py:29
  73.3 41.6 %all-to-all-done = bf16[32,30,16,128]{3,2,1,0:T(8,128)(2,1)} async-done(((bf16[32,30,16,128]{3,2,1,0:T(8,128)(2,1)}), bf16[32,30,16,128]{3,2,1,0:T(8,128)(2,1)}, u32[]{:S(2)}, u32[]{:S(2)}) %all-to-all-start) | async-done | bytes 3932192 | tf_op jit(solution)/shard_map/all_to_all | solution.py:283
  119.9 3.9 %collective-permute-done.5.refs_6_ = bf16[3,96,2048]{2,1,0:T(8,128)(2,1)} collective-permute-done((bf16[3,96,2048]{2,1,0:T(8,128)(2,1)}, bf16[3,96,2048]{2,1,0:T(8,128)(2,1)}, u32[]{:S(2)}, u32[]{:S(2)}) %collective-permute-start.5) | collective-permute-done | bytes 1179680 | tf_op jit(solution)/shard_map/ppermute | solution.py:29
  123.8 13.6 %expert_pass.2 = (bf16[320,2048]{1,0:T(8,128)(2,1)}, bf16[4,320,384]{2,1,0:T(8,128)(2,1)}) custom-call(bf16[320,2048]{1,0:T(8,128)(2,1)} %bitcast.169, bf16[320,2048]{1,0:T(8,128)(2,1)} %bitcast.179, bf16[3,96,2048]{2,1,0:T(8,128)(2,1)} %layer_part.3.refs_0_, bf16[3,96,2048]{2,1,0:T(8,128)(2,1)} %layer_part.4.refs_1_, ...), custom_call_target="tpu_custom_call" | custom-call | flops 5033164800 | bytes 13369344 | tf_op jit(solution)/shard_map/expert_pass/pallas_call | solution.py:192
  137.5 2.7 copy.27
  140.1 9.4 %all-to-all-start.1 = ((bf16[32,10,16,128]{3,2,1,0:T(8,128)(2,1)}), bf16[32,10,16,128]{3,2,1,0:T(8,128)(2,1)S(1)}, u32[]{:S(2)}, u32[]{:S(2)}) async-start(bf16[32,10,16,128]{3,2,1,0:T(8,128)(2,1)} %bitcast.42), calls=%async_computation.1 | async-start | bytes 2621440 | tf_op jit(solution)/shard_map/all_to_all | solution.py:291
  149.6 4.3 %layer_part.5.refs_0_ = bf16[3,192,2048]{2,1,0:T(8,128)(2,1)} custom-call(s32[1]{0:T(128)} %bitcast.10.index_ref, bf16[3,192,2048]{2,1,0:T(8,128)(2,1)} %copy-done, bf16[2,192,2048]{2,1,0:T(8,128)(2,1)} %bitcast.158, bf16[2,192,2048]{2,1,0:T(8,128)(2,1)} %bitcast.162, bf16[2,192,2048]{2,1,0:T(8,128)(2,1)} %bitcast.166), custom_call_target="tpu_custom_call" | custom-call | tf_op jit(solution)/shard_map/layer_part/pallas_call | solution.py:83
  153.8 2.7 collective-permute-start.9
  156.5 24.2 %all-to-all-done.1 = bf16[32,10,16,128]{3,2,1,0:T(8,128)(2,1)S(1)} async-done(((bf16[32,10,16,128]{3,2,1,0:T(8,128)(2,1)}), bf16[32,10,16,128]{3,2,1,0:T(8,128)(2,1)S(1)}, u32[]{:S(2)}, u32[]{:S(2)}) %all-to-all-start.1) | async-done | bytes 1310752 | tf_op jit(solution)/shard_map/all_to_all | solution.py:291
  181.2 4.2 %collective-permute-start.7 = (f32[64,2048]{1,0:T(8,128)S(1)}, f32[64,2048]{1,0:T(8,128)S(1)}, u32[]{:S(2)}, u32[]{:S(2)}) collective-permute-start(f32[64,2048]{1,0:T(8,128)S(1)} %fusion.9), channel_id=1, source_target_pairs={{0,128},{128,0},{1,129},{129,1},{2,130},{130,2},{3,131},{131,3},{4... | collective-permute-start | bytes 1572872 | tf_op jit(solution)/shard_map/ppermute | solution.py:20
  189.3 4.8 %all-to-all-start.2 = ((bf16[32,10,16,128]{3,2,1,0:T(8,128)(2,1)}), bf16[32,10,16,128]{3,2,1,0:T(8,128)(2,1)S(1)}, u32[]{:S(2)}, u32[]{:S(2)}) async-start(bf16[32,10,16,128]{3,2,1,0:T(8,128)(2,1)} %bitcast.51), calls=%async_computation.2 | async-start | bytes 2621440 | tf_op jit(solution)/shard_map/all_to_all | solution.py:133
  194.0 12.3 %collective-permute-done.8.refs_1_ = bf16[3,192,2048]{2,1,0:T(8,128)(2,1)} collective-permute-done((bf16[3,192,2048]{2,1,0:T(8,128)(2,1)}, bf16[3,192,2048]{2,1,0:T(8,128)(2,1)}, u32[]{:S(2)}, u32[]{:S(2)}) %collective-permute-start.8) | collective-permute-done | bytes 2359328 | tf_op jit(solution)/shard_map/ppermute | solution.py:29
  210.3 2.6 collective-permute-start.11
  216.7 17.3 %collective-permute-done.10.refs_3_ = bf16[3,96,2048]{2,1,0:T(8,128)(2,1)} collective-permute-done((bf16[3,96,2048]{2,1,0:T(8,128)(2,1)S(1)}, bf16[3,96,2048]{2,1,0:T(8,128)(2,1)}, u32[]{:S(2)}, u32[]{:S(2)}) %collective-permute-start.10) | collective-permute-done | bytes 1179680 | tf_op jit(solution)/shard_map/ppermute | solution.py:29
  235.6 3.4 %collective-permute-start.16 = (bf16[320,2048]{1,0:T(8,128)(2,1)S(1)}, bf16[320,2048]{1,0:T(8,128)(2,1)S(1)}, u32[]{:S(2)}, u32[]{:S(2)}) collective-permute-start(bf16[320,2048]{1,0:T(8,128)(2,1)S(1)} %broadcast_select_fusion), channel_id=1, source_target_pairs={{0,3},{1,0},{2,1},{3,2},{4,7},{5,4},{6,5},{7,6},{8,11},{9,8},{10,9... | collective-permute-start | bytes 3932168 | tf_op jit(solution)/shard_map/ppermute | solution.py:29
  239.1 25.4 %collective-permute-done.14 = bf16[320,2048]{1,0:T(8,128)(2,1)S(1)} collective-permute-done((bf16[320,2048]{1,0:T(8,128)(2,1)S(1)}, bf16[320,2048]{1,0:T(8,128)(2,1)S(1)}, u32[]{:S(2)}, u32[]{:S(2)}) %collective-permute-start.14) | collective-permute-done | bytes 1310752 | tf_op jit(solution)/shard_map/ppermute | solution.py:29
  266.3 2.7 collective-permute-start.19
  270.4 13.6 %expert_pass.3 = (bf16[320,2048]{1,0:T(8,128)(2,1)}, bf16[4,320,384]{2,1,0:T(8,128)(2,1)}) custom-call(bf16[320,2048]{1,0:T(8,128)(2,1)} %bitcast.173, bf16[320,2048]{1,0:T(8,128)(2,1)} %bitcast.181, bf16[3,192,2048]{2,1,0:T(8,128)(2,1)} %layer_part.5.refs_0_, bf16[3,192,2048]{2,1,0:T(8,128)(2,1)} %collective-permute-done.8.refs_1_, ...), custom_call_target="tpu_custom_call" | custom-call | flops 5033164800 | bytes 13369344 | tf_op jit(solution)/shard_map/expert_pass/pallas_call | solution.py:192
  284.0 2.7 copy.32
  286.7 8.6 %all-to-all-start.3 = ((bf16[32,10,16,128]{3,2,1,0:T(8,128)(2,1)}), bf16[32,10,16,128]{3,2,1,0:T(8,128)(2,1)}, u32[]{:S(2)}, u32[]{:S(2)}) async-start(bf16[32,10,16,128]{3,2,1,0:T(8,128)(2,1)} %bitcast.57), calls=%async_computation.3 | async-start | bytes 2621440 | tf_op jit(solution)/shard_map/all_to_all | solution.py:291
  296.9 2.7 collective-permute-start.15
  300.6 2.6 collective-permute-done.13
  309.2 6.6 %collective-permute-start.20 = (bf16[384,2048]{1,0:T(8,128)(2,1)S(1)}, bf16[384,2048]{1,0:T(8,128)(2,1)}, u32[]{:S(2)}, u32[]{:S(2)}) collective-permute-start(bf16[384,2048]{1,0:T(8,128)(2,1)S(1)} %add_convert_fusion), channel_id=1, source_target_pairs={{0,128},{128,0},{1,129},{129,1},{2,130},{130,2},{3,131},{131,3},{4... | collective-permute-start | bytes 4718600 | tf_op jit(solution)/shard_map/ppermute | solution.py:20
  315.8 3.2 collective-permute-done.20
  319.0 2.9 select_bitcast_fusion.1
  323.7 8.4 %collective-permute-start.12 = (f32[64,2048]{1,0:T(8,128)S(1)}, f32[64,2048]{1,0:T(8,128)S(1)}, u32[]{:S(2)}, u32[]{:S(2)}) collective-permute-start(f32[64,2048]{1,0:T(8,128)S(1)} %fusion.6), channel_id=1, source_target_pairs={{0,128},{128,0},{1,129},{129,1},{2,130},{130,2},{3,131},{131,3},{4... | collective-permute-start | bytes 1572872 | tf_op jit(solution)/shard_map/ppermute | solution.py:20
  (136 shorter events, 60.8 us)
Async XLA Ops:
  0.6 8.7 %copy-start.11 = (bf16[64,2048]{1,0:T(8,128)(2,1)S(1)}, bf16[64,2048]{1,0:T(8,128)(2,1)}, u32[]{:S(2)}) copy-start(bf16[64,2048]{1,0:T(8,128)(2,1)} %param.16) | copy-start | bytes 786436
  17.4 97.4 %all-to-all-start = ((bf16[32,30,16,128]{3,2,1,0:T(8,128)(2,1)}), bf16[32,30,16,128]{3,2,1,0:T(8,128)(2,1)}, u32[]{:S(2)}, u32[]{:S(2)}) async-start(bf16[32,30,16,128]{3,2,1,0:T(8,128)(2,1)} %pad_maximum_fusion), calls=%async_computation | async-start | bytes 7864320 | tf_op jit(solution)/shard_map/all_to_all | solution.py:283
  31.0 5.0 %collective-permute-start = (bf16[3,192,2048]{2,1,0:T(8,128)(2,1)}, bf16[3,192,2048]{2,1,0:T(8,128)(2,1)S(1)}, u32[]{:S(2)}, u32[]{:S(2)}) collective-permute-start(bf16[3,192,2048]{2,1,0:T(8,128)(2,1)} %expert_part.1), channel_id=1, source_target_pairs={{0,128},{128,0},{1,129},{129,1},{2,130},{130,2},{3,131},{131,3},{4... | collective-permute-start | bytes 7077896 | tf_op jit(solution)/shard_map/ppermute | solution.py:20
  39.9 27.8 %collective-permute-start.4 = (bf16[3,96,2048]{2,1,0:T(8,128)(2,1)}, bf16[3,96,2048]{2,1,0:T(8,128)(2,1)S(1)}, u32[]{:S(2)}, u32[]{:S(2)}) collective-permute-start(bf16[3,96,2048]{2,1,0:T(8,128)(2,1)} %layer_part.4.refs_1_), channel_id=1, source_target_pairs={{0,3},{1,0},{2,1},{3,2},{4,7},{5,4},{6,5},{7,6},{8,11},{9,8},{10,9... | collective-permute-start | bytes 3538952 | tf_op jit(solution)/shard_map/ppermute | solution.py:29
  44.9 28.4 %collective-permute-start.1 = (bf16[3,96,2048]{2,1,0:T(8,128)(2,1)}, bf16[3,96,2048]{2,1,0:T(8,128)(2,1)}, u32[]{:S(2)}, u32[]{:S(2)}) collective-permute-start(bf16[3,96,2048]{2,1,0:T(8,128)(2,1)} %layer_part.3.refs_0_), channel_id=1, source_target_pairs={{0,1},{1,2},{2,3},{3,0},{4,5},{5,6},{6,7},{7,4},{8,9},{9,10},{10,1... | collective-permute-start | bytes 3538952 | tf_op jit(solution)/shard_map/ppermute | solution.py:29
  44.9 75.0 %collective-permute-start.2 = (bf16[3,96,2048]{2,1,0:T(8,128)(2,1)S(1)}, bf16[3,96,2048]{2,1,0:T(8,128)(2,1)}, u32[]{:S(2)}, u32[]{:S(2)}) collective-permute-start(bf16[3,96,2048]{2,1,0:T(8,128)(2,1)S(1)} %copy-done.10), channel_id=1, source_target_pairs={{0,1},{1,2},{2,3},{3,0},{4,5},{5,6},{6,7},{7,4},{8,9},{9,10},{10,1... | collective-permute-start | bytes 3538952 | tf_op jit(solution)/shard_map/ppermute | solution.py:29
  45.2 74.7 %collective-permute-start.3 = (bf16[3,96,2048]{2,1,0:T(8,128)(2,1)}, bf16[3,96,2048]{2,1,0:T(8,128)(2,1)}, u32[]{:S(2)}, u32[]{:S(2)}) collective-permute-start(bf16[3,96,2048]{2,1,0:T(8,128)(2,1)} %layer_part.3.refs_0_), channel_id=1, source_target_pairs={{0,3},{1,0},{2,1},{3,2},{4,7},{5,4},{6,5},{7,6},{8,11},{9,8},{10,9... | collective-permute-start | bytes 3538952 | tf_op jit(solution)/shard_map/ppermute | solution.py:29
  67.6 49.4 %copy-start.15 = (bf16[3,96,2048]{2,1,0:T(8,128)(2,1)}, bf16[3,96,2048]{2,1,0:T(8,128)(2,1)S(1)}, u32[]{:S(2)}) copy-start(bf16[3,96,2048]{2,1,0:T(8,128)(2,1)S(1)} %collective-permute-done.4.refs_5_) | copy-start | bytes 3538948
  67.6 52.2 %collective-permute-start.6 = (bf16[3,96,2048]{2,1,0:T(8,128)(2,1)S(1)}, bf16[3,96,2048]{2,1,0:T(8,128)(2,1)}, u32[]{:S(2)}, u32[]{:S(2)}) collective-permute-start(bf16[3,96,2048]{2,1,0:T(8,128)(2,1)S(1)} %collective-permute-done.4.refs_5_), channel_id=1, source_target_pairs={{0,3},{1,0},{2,1},{3,2},{4,7},{5,4},{6,5},{7,6},{8,11},{9,8},{10,9... | collective-permute-start | bytes 3538952 | tf_op jit(solution)/shard_map/ppermute | solution.py:29
  73.3 50.6 %collective-permute-start.5 = (bf16[3,96,2048]{2,1,0:T(8,128)(2,1)}, bf16[3,96,2048]{2,1,0:T(8,128)(2,1)}, u32[]{:S(2)}, u32[]{:S(2)}) collective-permute-start(bf16[3,96,2048]{2,1,0:T(8,128)(2,1)} %collective-permute-done.1.refs_2_), channel_id=1, source_target_pairs={{0,1},{1,2},{2,3},{3,0},{4,5},{5,6},{6,7},{7,4},{8,9},{9,10},{10,1... | collective-permute-start | bytes 3538952 | tf_op jit(solution)/shard_map/ppermute | solution.py:29
  140.1 40.6 %all-to-all-start.1 = ((bf16[32,10,16,128]{3,2,1,0:T(8,128)(2,1)}), bf16[32,10,16,128]{3,2,1,0:T(8,128)(2,1)S(1)}, u32[]{:S(2)}, u32[]{:S(2)}) async-start(bf16[32,10,16,128]{3,2,1,0:T(8,128)(2,1)} %bitcast.42), calls=%async_computation.1 | async-start | bytes 2621440 | tf_op jit(solution)/shard_map/all_to_all | solution.py:291
  153.8 52.5 %collective-permute-start.8 = (bf16[3,192,2048]{2,1,0:T(8,128)(2,1)}, bf16[3,192,2048]{2,1,0:T(8,128)(2,1)}, u32[]{:S(2)}, u32[]{:S(2)}) collective-permute-start(bf16[3,192,2048]{2,1,0:T(8,128)(2,1)} %layer_part.5.refs_0_), channel_id=1, source_target_pairs={{0,1},{1,2},{2,3},{3,0},{4,5},{5,6},{6,7},{7,4},{8,9},{9,10},{10,1... | collective-permute-start | bytes 7077896 | tf_op jit(solution)/shard_map/ppermute | solution.py:29
  153.8 54.0 %collective-permute-start.9 = (bf16[3,192,2048]{2,1,0:T(8,128)(2,1)}, bf16[3,192,2048]{2,1,0:T(8,128)(2,1)}, u32[]{:S(2)}, u32[]{:S(2)}) collective-permute-start(bf16[3,192,2048]{2,1,0:T(8,128)(2,1)} %layer_part.5.refs_0_), channel_id=1, source_target_pairs={{0,3},{1,0},{2,1},{3,2},{4,7},{5,4},{6,5},{7,6},{8,11},{9,8},{10,9... | collective-permute-start | bytes 7077896 | tf_op jit(solution)/shard_map/ppermute | solution.py:29
  181.2 6.0 %copy-start.12 = (bf16[64,2048]{1,0:T(8,128)(2,1)S(1)}, bf16[64,2048]{1,0:T(8,128)(2,1)}, u32[]{:S(2)}) copy-start(bf16[64,2048]{1,0:T(8,128)(2,1)} %param.16) | copy-start | bytes 786436
  181.2 5.7 %collective-permute-start.7 = (f32[64,2048]{1,0:T(8,128)S(1)}, f32[64,2048]{1,0:T(8,128)S(1)}, u32[]{:S(2)}, u32[]{:S(2)}) collective-permute-start(f32[64,2048]{1,0:T(8,128)S(1)} %fusion.9), channel_id=1, source_target_pairs={{0,128},{128,0},{1,129},{129,1},{2,130},{130,2},{3,131},{131,3},{4... | collective-permute-start | bytes 1572872 | tf_op jit(solution)/shard_map/ppermute | solution.py:20
  189.3 79.7 %all-to-all-start.2 = ((bf16[32,10,16,128]{3,2,1,0:T(8,128)(2,1)}), bf16[32,10,16,128]{3,2,1,0:T(8,128)(2,1)S(1)}, u32[]{:S(2)}, u32[]{:S(2)}) async-start(bf16[32,10,16,128]{3,2,1,0:T(8,128)(2,1)} %bitcast.51), calls=%async_computation.2 | async-start | bytes 2621440 | tf_op jit(solution)/shard_map/all_to_all | solution.py:133
  207.7 26.3 %collective-permute-start.10 = (bf16[3,96,2048]{2,1,0:T(8,128)(2,1)S(1)}, bf16[3,96,2048]{2,1,0:T(8,128)(2,1)}, u32[]{:S(2)}, u32[]{:S(2)}) collective-permute-start(bf16[3,96,2048]{2,1,0:T(8,128)(2,1)S(1)} %slice.116), channel_id=1, source_target_pairs={{0,1},{1,2},{2,3},{3,0},{4,5},{5,6},{6,7},{7,4},{8,9},{9,10},{10,1... | collective-permute-start | bytes 3538952 | tf_op jit(solution)/shard_map/ppermute | solution.py:29
  210.3 25.4 %collective-permute-start.11 = (bf16[3,96,2048]{2,1,0:T(8,128)(2,1)}, bf16[3,96,2048]{2,1,0:T(8,128)(2,1)}, u32[]{:S(2)}, u32[]{:S(2)}) collective-permute-start(bf16[3,96,2048]{2,1,0:T(8,128)(2,1)} %slice.117), channel_id=1, source_target_pairs={{0,3},{1,0},{2,1},{3,2},{4,7},{5,4},{6,5},{7,6},{8,11},{9,8},{10,9... | collective-permute-start | bytes 3538952 | tf_op jit(solution)/shard_map/ppermute | solution.py:29
  216.6 49.6 %copy-start.3 = (bf16[320,2048]{1,0:T(8,128)(2,1)}, bf16[320,2048]{1,0:T(8,128)(2,1)S(1)}, u32[]{:S(2)}) copy-start(bf16[320,2048]{1,0:T(8,128)(2,1)S(1)} %broadcast_select_fusion) | copy-start | bytes 3932164
  235.6 28.8 %collective-permute-start.14 = (bf16[320,2048]{1,0:T(8,128)(2,1)S(1)}, bf16[320,2048]{1,0:T(8,128)(2,1)S(1)}, u32[]{:S(2)}, u32[]{:S(2)}) collective-permute-start(bf16[320,2048]{1,0:T(8,128)(2,1)S(1)} %broadcast_select_fusion), channel_id=1, source_target_pairs={{0,1},{1,2},{2,3},{3,0},{4,5},{5,6},{6,7},{7,4},{8,9},{9,10},{10,1... | collective-permute-start | bytes 3932168 | tf_op jit(solution)/shard_map/ppermute | solution.py:29
  235.6 29.8 %collective-permute-start.16 = (bf16[320,2048]{1,0:T(8,128)(2,1)S(1)}, bf16[320,2048]{1,0:T(8,128)(2,1)S(1)}, u32[]{:S(2)}, u32[]{:S(2)}) collective-permute-start(bf16[320,2048]{1,0:T(8,128)(2,1)S(1)} %broadcast_select_fusion), channel_id=1, source_target_pairs={{0,3},{1,0},{2,1},{3,2},{4,7},{5,4},{6,5},{7,6},{8,11},{9,8},{10,9... | collective-permute-start | bytes 3932168 | tf_op jit(solution)/shard_map/ppermute | solution.py:29
  265.4 40.9 %collective-permute-start.18 = (bf16[160,2048]{1,0:T(8,128)(2,1)}, bf16[160,2048]{1,0:T(8,128)(2,1)}, u32[]{:S(2)}, u32[]{:S(2)}) collective-permute-start(bf16[160,2048]{1,0:T(8,128)(2,1)} %slice.118), channel_id=1, source_target_pairs={{0,1},{1,2},{2,3},{3,0},{4,5},{5,6},{6,7},{7,4},{8,9},{9,10},{10,1... | collective-permute-start | bytes 1966088 | tf_op jit(solution)/shard_map/ppermute | solution.py:29
  266.3 40.0 %collective-permute-start.19 = (bf16[160,2048]{1,0:T(8,128)(2,1)}, bf16[160,2048]{1,0:T(8,128)(2,1)}, u32[]{:S(2)}, u32[]{:S(2)}) collective-permute-start(bf16[160,2048]{1,0:T(8,128)(2,1)} %slice.119), channel_id=1, source_target_pairs={{0,3},{1,0},{2,1},{3,2},{4,7},{5,4},{6,5},{7,6},{8,11},{9,8},{10,9... | collective-permute-start | bytes 1966088 | tf_op jit(solution)/shard_map/ppermute | solution.py:29
  286.7 8.6 %copy-start.13 = (bf16[4,320,384]{2,1,0:T(8,128)(2,1)S(1)}, bf16[4,320,384]{2,1,0:T(8,128)(2,1)}, u32[]{:S(2)}) copy-start(bf16[4,320,384]{2,1,0:T(8,128)(2,1)} %get-tuple-element.19) | copy-start | bytes 2949124
  286.7 35.1 %all-to-all-start.3 = ((bf16[32,10,16,128]{3,2,1,0:T(8,128)(2,1)}), bf16[32,10,16,128]{3,2,1,0:T(8,128)(2,1)}, u32[]{:S(2)}, u32[]{:S(2)}) async-start(bf16[32,10,16,128]{3,2,1,0:T(8,128)(2,1)} %bitcast.57), calls=%async_computation.3 | async-start | bytes 2621440 | tf_op jit(solution)/shard_map/all_to_all | solution.py:291
  296.8 6.3 %collective-permute-start.13 = (bf16[320,384]{1,0:T(8,128)(2,1)S(1)}, bf16[320,384]{1,0:T(8,128)(2,1)S(1)}, u32[]{:S(2)}, u32[]{:S(2)}) collective-permute-start(bf16[320,384]{1,0:T(8,128)(2,1)S(1)} %get-tuple-element.43), channel_id=1, source_target_pairs={{0,1},{1,2},{2,3},{3,0},{4,5},{5,6},{6,7},{7,4},{8,9},{9,10},{10,1... | collective-permute-start | bytes 737288 | tf_op jit(solution)/shard_map/ppermute | solution.py:29
  296.9 8.4 %collective-permute-start.15 = (bf16[320,384]{1,0:T(8,128)(2,1)S(1)}, bf16[320,384]{1,0:T(8,128)(2,1)S(1)}, u32[]{:S(2)}, u32[]{:S(2)}) collective-permute-start(bf16[320,384]{1,0:T(8,128)(2,1)S(1)} %get-tuple-element.42), channel_id=1, source_target_pairs={{0,3},{1,0},{2,1},{3,2},{4,7},{5,4},{6,5},{7,6},{8,11},{9,8},{10,9... | collective-permute-start | bytes 737288 | tf_op jit(solution)/shard_map/ppermute | solution.py:29
  299.5 7.2 %collective-permute-start.17 = (bf16[320,384]{1,0:T(8,128)(2,1)S(1)}, bf16[320,384]{1,0:T(8,128)(2,1)S(1)}, u32[]{:S(2)}, u32[]{:S(2)}) collective-permute-start(bf16[320,384]{1,0:T(8,128)(2,1)S(1)} %get-tuple-element.41), channel_id=1, source_target_pairs={{0,2},{1,3},{2,0},{3,1},{4,6},{5,7},{6,4},{7,5},{8,10},{9,11},{10,... | collective-permute-start | bytes 737288 | tf_op jit(solution)/shard_map/ppermute | solution.py:29
  309.2 9.8 %collective-permute-start.20 = (bf16[384,2048]{1,0:T(8,128)(2,1)S(1)}, bf16[384,2048]{1,0:T(8,128)(2,1)}, u32[]{:S(2)}, u32[]{:S(2)}) collective-permute-start(bf16[384,2048]{1,0:T(8,128)(2,1)S(1)} %add_convert_fusion), channel_id=1, source_target_pairs={{0,128},{128,0},{1,129},{129,1},{2,130},{130,2},{3,131},{131,3},{4... | collective-permute-start | bytes 4718600 | tf_op jit(solution)/shard_map/ppermute | solution.py:20
  321.8 10.3 %copy-start.6 = (bf16[1,1,192,2048]{3,2,1,0:T(8,128)(2,1)S(1)}, bf16[1,1,192,2048]{3,2,1,0:T(8,128)(2,1)}, u32[]{:S(2)}) copy-start(bf16[1,1,192,2048]{3,2,1,0:T(8,128)(2,1)} %get-tuple-element.37) | copy-start | bytes 2359300
  321.8 10.3 %copy-start.7 = (bf16[1,1,192,2048]{3,2,1,0:T(8,128)(2,1)S(1)}, bf16[1,1,192,2048]{3,2,1,0:T(8,128)(2,1)}, u32[]{:S(2)}) copy-start(bf16[1,1,192,2048]{3,2,1,0:T(8,128)(2,1)} %get-tuple-element.39) | copy-start | bytes 2359300
  323.7 12.5 %collective-permute-start.12 = (f32[64,2048]{1,0:T(8,128)S(1)}, f32[64,2048]{1,0:T(8,128)S(1)}, u32[]{:S(2)}, u32[]{:S(2)}) collective-permute-start(f32[64,2048]{1,0:T(8,128)S(1)} %fusion.6), channel_id=1, source_target_pairs={{0,128},{128,0},{1,129},{129,1},{2,130},{130,2},{3,131},{131,3},{4... | collective-permute-start | bytes 1572872 | tf_op jit(solution)/shard_map/ppermute | solution.py:20
  (9 other events, 20.2 us)

commit v2 on v1

--- a/solution.py
+++ b/solution.py
@@ -94,6 +94,48 @@
     )(index, got, *weights)
 
 
+def deliver_kernel(flags_ref, mine_ref, theirs_ref, gate_ref, up_ref):
+    units = gate_ref.shape[2]
+    own = flags_ref[0] == pl.program_id(0)
+    trained = flags_ref[1] == 1
+
+    def fill(part_ref):
+        gate_ref[0, 0] = part_ref[:units].astype(jnp.float32)
+        up_ref[0, 0] = part_ref[units:].astype(jnp.float32)
+
+    @pl.when(jnp.logical_and(trained, own))
+    def _():
+        fill(mine_ref)
+
+    @pl.when(jnp.logical_and(trained, jnp.logical_not(own)))
+    def _():
+        fill(theirs_ref)
+
+    @pl.when(jnp.logical_not(trained))
+    def _():
+        gate_ref[...] = jnp.zeros_like(gate_ref)
+        up_ref[...] = jnp.zeros_like(up_ref)
+
+
+def deliver(section, trained, mine, theirs):
+    both, width = mine.shape
+    flags = jnp.stack([section.astype(jnp.int32), trained.astype(jnp.int32)])
+    whole = pl.BlockSpec((both, width), lambda i, flags_ref: (0, 0))
+    one = pl.BlockSpec((1, 1, both // 2, width), lambda i, flags_ref: (0, i, 0, 0))
+    shape = jax.ShapeDtypeStruct((1, 2, both // 2, width), jnp.float32)
+    return pl.pallas_call(
+        deliver_kernel,
+        grid_spec=pltpu.PrefetchScalarGridSpec(
+            num_scalar_prefetch=1,
+            grid=(2,),
+            in_specs=[whole, whole],
+            out_specs=(one, one),
+        ),
+        out_shape=(shape, shape),
+        name="deliver",
+    )(flags, mine, theirs)
+
+
 def normalize(inputs, gain_vector):
     values = inputs.astype(jnp.float32)
     factor = lax.rsqrt(jnp.mean(values * values, axis=1, keepdims=True) + epsilon)
@@ -219,7 +261,12 @@
     top_count = routes.shape[2]
 
     stored = (w_gate[0], w_up[0], w_down[0])
-    index = section.astype(jnp.int32).reshape(1)
+    small = jnp.concatenate(
+        [norm_gain[0], routes[0].astype(jnp.float32).reshape(-1), probs[0].reshape(-1)]
+    )
+    small_parts = lax.all_gather(small, "section", axis=0)
+    input_parts = lax.all_gather(layer_inputs[0], "section", axis=0)
+    index = after(section.astype(jnp.int32).reshape(1), small_parts, input_parts)
     got = other_core(expert_part(1 - index, stored, 4))
     head1 = layer_part(1, 0, 2, 4, index, got, stored)
     tail1 = layer_part(1, 2, 2, 4, index, got, stored)
@@ -229,11 +276,6 @@
     head_behind = turned(head1, -1)
     head_far = turned(head_before, 1)
     tail_far = turned(tail_behind, -1)
-    small = jnp.concatenate(
-        [norm_gain[0], routes[0].astype(jnp.float32).reshape(-1), probs[0].reshape(-1)]
-    )
-    small_parts = lax.all_gather(small, "section", axis=0)
-    input_parts = lax.all_gather(layer_inputs[0], "section", axis=0)
     own0 = layer_part(0, 0, 4, 4, index, after(got, tail1), stored)
     before0, behind0 = ring_first(after(own0, head_far, tail_far))
     far0 = ring_second(before0, behind0)
@@ -314,7 +356,6 @@
     input_grad0 = finish(0, sent0, input_grad1)
     result = jnp.where(upper, input_grad1, input_grad0)
 
-    units = w_gate.shape[2]
     d_both = after(jnp.where(trained1, d_both1, d_both0), sent0)
     d_behind = turned(d_both[1], -1)
     d_before = turned(d_both[2], 1)
@@ -327,14 +368,7 @@
     from_other = other_core(grads)
     trained = sampled[0] == section
 
-    def on_owner(mine, theirs):
-        low = jnp.where(upper, theirs, mine)
-        high = jnp.where(upper, mine, theirs)
-        pair = jnp.stack([low, high]).astype(jnp.float32)
-        return jnp.where(trained, pair, 0.0)[None]
-
-    gate_share = on_owner(grads[:units], from_other[:units])
-    up_share = on_owner(grads[units:], from_other[units:])
+    gate_share, up_share = deliver(section, trained, grads, from_other)
     return (result[None], gate_share, up_share)
 
 

time: 339 us -> 341 us (level)
  other arithmetic: 14.6 us -> 8.15 us
  Pallas kernels: 40.4 us -> 45.8 us
    pallas_call x0 -> x1, Pallas kernels: none -> 5.47 us  [deliver(): pl.pallas_call(deliver_kernel, grid_spec=pltpu.PrefetchScalarGridSpec(num...]
    all_to_all x2, waiting for transfers between devices: 24.2 us -> 28.4 us  [finish(): lax.all_to_all(sent, 'expert', split_axis=0, concat_axis=0, tiled=True)]
    select_n x2 -> x0, other arithmetic: 4.08 us -> none  [on_owner(): return jnp.where(trained, pair, 0.0)[None]]
    unnamed x43 -> x39, local copies, waits for them, and re-layouts: 16 us -> 16 us
  transfers between devices with their start and end apart: 25 -> 25, of which waited for: 15 -> 15; matrix products, arithmetic and copies ran while one was open for 10% -> 9% of each run, Pallas kernels for 8% -> 10%
where the time goes in v2:
time: 341 us; the launch traced here: 339 us
  waiting for transfers between devices  163 us (48%)
  starting transfers between devices  77 us (23%)
  Pallas kernels  45.8 us (13%)
  local copies, waits for them, and re-layouts  26.9 us (8%)
  matrix products  10.1 us (3%)
  other arithmetic  8.15 us (2%)
  blocking collectives  6.83 us (2%)
    ppermute x17, waiting for transfers between devices, turned(): lax.ppermute(value, 'mp', [(i, (i + by) % peers) for i in range(peers)])  86.7 us
    all_to_all x1, waiting for transfers between devices, per_device(): lax.all_to_all(first, 'expert', split_axis=0, concat_axis=0, tiled=True)  42 us
    all_to_all x2, waiting for transfers between devices, finish(): lax.all_to_all(sent, 'expert', split_axis=0, concat_axis=0, tiled=True)  28.4 us
    pallas_call x2, Pallas kernels, expert_pass(): pl.pallas_call(functools.partial(expert_kernel, len(pieces)), in_specs=[v...  27.2 us
    ppermute x17, starting transfers between devices, turned(): lax.ppermute(value, 'mp', [(i, (i + by) % peers) for i in range(peers)])  22.9 us
    ppermute x4, starting transfers between devices, other_core(): return lax.ppermute(value, 'section', [(0, 1), (1, 0)])  21.6 us
    all_to_all x2, starting transfers between devices, finish(): lax.all_to_all(sent, 'expert', split_axis=0, concat_axis=0, tiled=True)  18.1 us
    unnamed x39, local copies, waits for them, and re-layouts  16 us
  transfers between devices with their start and end apart: 25, of which 15 were waited for; matrix products, arithmetic and copies ran while one was open for 9% of the time, Pallas kernels for 10%

profile of v2, /device:TPU:1, one launch (start us, length us, event | category | flops | bytes accessed | tf_op | source)
XLA Modules:
  0.0 339.4 jit_solution(5597915163851897829)
XLA Ops:
  3.1 4.7 %all-gather = f32[6144]{0:T(1024)S(1)} all-gather(f32[3072]{0:T(1024)S(1)} %pad_maximum_fusion.1), channel_id=2, replica_groups=mesh['section'=2,'expert'=32,'mp'=4] {'section'}, dimensions={0}, use_global_device_ids=true | all-gather | bytes 36864 | tf_op jit(solution)/shard_map/all_gather | solution.py:267
  17.4 9.6 %all-to-all-start = ((bf16[32,30,16,128]{3,2,1,0:T(8,128)(2,1)}), bf16[32,30,16,128]{3,2,1,0:T(8,128)(2,1)}, u32[]{:S(2)}, u32[]{:S(2)}) async-start(bf16[32,30,16,128]{3,2,1,0:T(8,128)(2,1)} %pad_maximum_fusion), calls=%async_computation | async-start | bytes 7864320 | tf_op jit(solution)/shard_map/all_to_all | solution.py:325
  27.1 3.9 %expert_part.1 = bf16[3,192,2048]{2,1,0:T(8,128)(2,1)} custom-call(s32[1]{0:T(128)S(6)} %sub.9.index_ref, bf16[2,192,2048]{2,1,0:T(8,128)(2,1)} %bitcast.148, bf16[2,192,2048]{2,1,0:T(8,128)(2,1)} %bitcast.152, bf16[2,192,2048]{2,1,0:T(8,128)(2,1)} %bitcast.156), custom_call_target="tpu_custom_call" | custom-call | tf_op jit(solution)/shard_map/expert_part/pallas_call | solution.py:54
  31.6 4.4 %collective-permute-done.got_ref = bf16[3,192,2048]{2,1,0:T(8,128)(2,1)S(1)} collective-permute-done((bf16[3,192,2048]{2,1,0:T(8,128)(2,1)}, bf16[3,192,2048]{2,1,0:T(8,128)(2,1)S(1)}, u32[]{:S(2)}, u32[]{:S(2)}) %collective-permute-start) | collective-permute-done | bytes 2359328 | tf_op jit(solution)/shard_map/ppermute | solution.py:20
  37.4 2.5 layer_part.4.refs_1_
  47.6 20.0 %collective-permute-done.4.refs_5_ = bf16[3,96,2048]{2,1,0:T(8,128)(2,1)S(1)} collective-permute-done((bf16[3,96,2048]{2,1,0:T(8,128)(2,1)}, bf16[3,96,2048]{2,1,0:T(8,128)(2,1)S(1)}, u32[]{:S(2)}, u32[]{:S(2)}) %collective-permute-start.4) | collective-permute-done | bytes 1179680 | tf_op jit(solution)/shard_map/ppermute | solution.py:29
  67.7 3.4 %collective-permute-start.6 = (bf16[3,96,2048]{2,1,0:T(8,128)(2,1)S(1)}, bf16[3,96,2048]{2,1,0:T(8,128)(2,1)}, u32[]{:S(2)}, u32[]{:S(2)}) collective-permute-start(bf16[3,96,2048]{2,1,0:T(8,128)(2,1)S(1)} %collective-permute-done.4.refs_5_), channel_id=1, source_target_pairs={{0,3},{1,0},{2,1},{3,2},{4,7},{5,4},{6,5},{7,6},{8,11},{9,8},{10,9... | collective-permute-start | bytes 3538952 | tf_op jit(solution)/shard_map/ppermute | solution.py:29
  73.3 42.0 %all-to-all-done = bf16[32,30,16,128]{3,2,1,0:T(8,128)(2,1)} async-done(((bf16[32,30,16,128]{3,2,1,0:T(8,128)(2,1)}), bf16[32,30,16,128]{3,2,1,0:T(8,128)(2,1)}, u32[]{:S(2)}, u32[]{:S(2)}) %all-to-all-start) | async-done | bytes 3932192 | tf_op jit(solution)/shard_map/all_to_all | solution.py:325
  120.3 3.5 %collective-permute-done.5.refs_6_ = bf16[3,96,2048]{2,1,0:T(8,128)(2,1)} collective-permute-done((bf16[3,96,2048]{2,1,0:T(8,128)(2,1)}, bf16[3,96,2048]{2,1,0:T(8,128)(2,1)}, u32[]{:S(2)}, u32[]{:S(2)}) %collective-permute-start.5) | collective-permute-done | bytes 1179680 | tf_op jit(solution)/shard_map/ppermute | solution.py:29
  123.8 13.6 %expert_pass.2 = (bf16[320,2048]{1,0:T(8,128)(2,1)}, bf16[4,320,384]{2,1,0:T(8,128)(2,1)}) custom-call(bf16[320,2048]{1,0:T(8,128)(2,1)} %bitcast.162, bf16[320,2048]{1,0:T(8,128)(2,1)} %bitcast.172, bf16[3,96,2048]{2,1,0:T(8,128)(2,1)} %layer_part.3.refs_0_, bf16[3,96,2048]{2,1,0:T(8,128)(2,1)} %layer_part.4.refs_1_, ...), custom_call_target="tpu_custom_call" | custom-call | flops 5033164800 | bytes 13369344 | tf_op jit(solution)/shard_map/expert_pass/pallas_call | solution.py:234
  137.4 2.7 copy.27
  140.1 9.4 %all-to-all-start.1 = ((bf16[32,10,16,128]{3,2,1,0:T(8,128)(2,1)}), bf16[32,10,16,128]{3,2,1,0:T(8,128)(2,1)S(1)}, u32[]{:S(2)}, u32[]{:S(2)}) async-start(bf16[32,10,16,128]{3,2,1,0:T(8,128)(2,1)} %bitcast.39), calls=%async_computation.1 | async-start | bytes 2621440 | tf_op jit(solution)/shard_map/all_to_all | solution.py:333
  149.5 4.3 %layer_part.5.refs_0_ = bf16[3,192,2048]{2,1,0:T(8,128)(2,1)} custom-call(s32[1]{0:T(128)} %bitcast.10.index_ref, bf16[3,192,2048]{2,1,0:T(8,128)(2,1)} %copy-done, bf16[2,192,2048]{2,1,0:T(8,128)(2,1)} %bitcast.151, bf16[2,192,2048]{2,1,0:T(8,128)(2,1)} %bitcast.155, bf16[2,192,2048]{2,1,0:T(8,128)(2,1)} %bitcast.159), custom_call_target="tpu_custom_call" | custom-call | tf_op jit(solution)/shard_map/layer_part/pallas_call | solution.py:83
  153.8 2.7 collective-permute-start.9
  156.5 24.2 %all-to-all-done.1 = bf16[32,10,16,128]{3,2,1,0:T(8,128)(2,1)S(1)} async-done(((bf16[32,10,16,128]{3,2,1,0:T(8,128)(2,1)}), bf16[32,10,16,128]{3,2,1,0:T(8,128)(2,1)S(1)}, u32[]{:S(2)}, u32[]{:S(2)}) %all-to-all-start.1) | async-done | bytes 1310752 | tf_op jit(solution)/shard_map/all_to_all | solution.py:333
  181.1 4.2 %collective-permute-start.7 = (f32[64,2048]{1,0:T(8,128)S(1)}, f32[64,2048]{1,0:T(8,128)S(1)}, u32[]{:S(2)}, u32[]{:S(2)}) collective-permute-start(f32[64,2048]{1,0:T(8,128)S(1)} %fusion.9), channel_id=1, source_target_pairs={{0,128},{128,0},{1,129},{129,1},{2,130},{130,2},{3,131},{131,3},{4... | collective-permute-start | bytes 1572872 | tf_op jit(solution)/shard_map/ppermute | solution.py:20
  189.2 4.8 %all-to-all-start.2 = ((bf16[32,10,16,128]{3,2,1,0:T(8,128)(2,1)}), bf16[32,10,16,128]{3,2,1,0:T(8,128)(2,1)S(1)}, u32[]{:S(2)}, u32[]{:S(2)}) async-start(bf16[32,10,16,128]{3,2,1,0:T(8,128)(2,1)} %bitcast.48), calls=%async_computation.2 | async-start | bytes 2621440 | tf_op jit(solution)/shard_map/all_to_all | solution.py:175
  194.0 12.3 %collective-permute-done.8.refs_1_ = bf16[3,192,2048]{2,1,0:T(8,128)(2,1)} collective-permute-done((bf16[3,192,2048]{2,1,0:T(8,128)(2,1)}, bf16[3,192,2048]{2,1,0:T(8,128)(2,1)}, u32[]{:S(2)}, u32[]{:S(2)}) %collective-permute-start.8) | collective-permute-done | bytes 2359328 | tf_op jit(solution)/shard_map/ppermute | solution.py:29
  210.2 2.6 collective-permute-start.11
  216.6 17.4 %collective-permute-done.10.refs_3_ = bf16[3,96,2048]{2,1,0:T(8,128)(2,1)} collective-permute-done((bf16[3,96,2048]{2,1,0:T(8,128)(2,1)S(1)}, bf16[3,96,2048]{2,1,0:T(8,128)(2,1)}, u32[]{:S(2)}, u32[]{:S(2)}) %collective-permute-start.10) | collective-permute-done | bytes 1179680 | tf_op jit(solution)/shard_map/ppermute | solution.py:29
  235.6 3.4 %collective-permute-start.16 = (bf16[320,2048]{1,0:T(8,128)(2,1)S(1)}, bf16[320,2048]{1,0:T(8,128)(2,1)S(1)}, u32[]{:S(2)}, u32[]{:S(2)}) collective-permute-start(bf16[320,2048]{1,0:T(8,128)(2,1)S(1)} %broadcast_select_fusion), channel_id=1, source_target_pairs={{0,3},{1,0},{2,1},{3,2},{4,7},{5,4},{6,5},{7,6},{8,11},{9,8},{10,9... | collective-permute-start | bytes 3932168 | tf_op jit(solution)/shard_map/ppermute | solution.py:29
  239.0 25.4 %collective-permute-done.14 = bf16[320,2048]{1,0:T(8,128)(2,1)S(1)} collective-permute-done((bf16[320,2048]{1,0:T(8,128)(2,1)S(1)}, bf16[320,2048]{1,0:T(8,128)(2,1)S(1)}, u32[]{:S(2)}, u32[]{:S(2)}) %collective-permute-start.14) | collective-permute-done | bytes 1310752 | tf_op jit(solution)/shard_map/ppermute | solution.py:29
  266.3 2.7 collective-permute-start.19
  270.4 13.6 %expert_pass.3 = (bf16[320,2048]{1,0:T(8,128)(2,1)}, bf16[4,320,384]{2,1,0:T(8,128)(2,1)}) custom-call(bf16[320,2048]{1,0:T(8,128)(2,1)} %bitcast.166, bf16[320,2048]{1,0:T(8,128)(2,1)} %bitcast.174, bf16[3,192,2048]{2,1,0:T(8,128)(2,1)} %layer_part.5.refs_0_, bf16[3,192,2048]{2,1,0:T(8,128)(2,1)} %collective-permute-done.8.refs_1_, ...), custom_call_target="tpu_custom_call" | custom-call | flops 5033164800 | bytes 13369344 | tf_op jit(solution)/shard_map/expert_pass/pallas_call | solution.py:234
  284.0 2.7 copy.32
  286.7 8.6 %all-to-all-start.3 = ((bf16[32,10,16,128]{3,2,1,0:T(8,128)(2,1)}), bf16[32,10,16,128]{3,2,1,0:T(8,128)(2,1)}, u32[]{:S(2)}, u32[]{:S(2)}) async-start(bf16[32,10,16,128]{3,2,1,0:T(8,128)(2,1)} %bitcast.54), calls=%async_computation.3 | async-start | bytes 2621440 | tf_op jit(solution)/shard_map/all_to_all | solution.py:333
  296.9 2.7 collective-permute-start.15
  300.6 2.6 collective-permute-done.13
  309.3 6.5 %collective-permute-start.20 = (bf16[384,2048]{1,0:T(8,128)(2,1)S(1)}, bf16[384,2048]{1,0:T(8,128)(2,1)}, u32[]{:S(2)}, u32[]{:S(2)}) collective-permute-start(bf16[384,2048]{1,0:T(8,128)(2,1)S(1)} %add_convert_fusion.mine_ref), channel_id=1, source_target_pairs={{0,128},{128,0},{1,129},{129,1},{2,130},{130,2},{3,131},{131,3},{4... | collective-permute-start | bytes 4718600 | tf_op jit(solution)/shard_map/ppermute | solution.py:20
  315.8 4.2 %all-to-all-done.3 = bf16[32,10,16,128]{3,2,1,0:T(8,128)(2,1)} async-done(((bf16[32,10,16,128]{3,2,1,0:T(8,128)(2,1)}), bf16[32,10,16,128]{3,2,1,0:T(8,128)(2,1)}, u32[]{:S(2)}, u32[]{:S(2)}) %all-to-all-start.3) | async-done | bytes 1310752 | tf_op jit(solution)/shard_map/all_to_all | solution.py:333
  321.8 10.3 %collective-permute-start.12 = (f32[64,2048]{1,0:T(8,128)S(1)}, f32[64,2048]{1,0:T(8,128)S(1)}, u32[]{:S(2)}, u32[]{:S(2)}) collective-permute-start(f32[64,2048]{1,0:T(8,128)S(1)} %fusion.6), channel_id=1, source_target_pairs={{0,128},{128,0},{1,129},{129,1},{2,130},{130,2},{3,131},{131,3},{4... | collective-permute-start | bytes 1572872 | tf_op jit(solution)/shard_map/ppermute | solution.py:20
  332.7 5.5 %deliver.1 = (f32[1,2,192,2048]{3,2,1,0:T(8,128)}, f32[1,2,192,2048]{3,2,1,0:T(8,128)}) custom-call(s32[2]{0:T(128)} %pad_add_fusion.flags_ref, bf16[384,2048]{1,0:T(8,128)(2,1)} %copy-done.1, bf16[384,2048]{1,0:T(8,128)(2,1)} %collective-permute-done.20.theirs_ref), custom_call_target="tpu_custom_call" | custom-call | tf_op jit(solution)/shard_map/deliver/pallas_call | solution.py:126
  (131 shorter events, 57.3 us)
Async XLA Ops:
  0.6 8.7 %copy-start.9 = (bf16[64,2048]{1,0:T(8,128)(2,1)S(1)}, bf16[64,2048]{1,0:T(8,128)(2,1)}, u32[]{:S(2)}) copy-start(bf16[64,2048]{1,0:T(8,128)(2,1)} %param.16) | copy-start | bytes 786436
  17.4 97.8 %all-to-all-start = ((bf16[32,30,16,128]{3,2,1,0:T(8,128)(2,1)}), bf16[32,30,16,128]{3,2,1,0:T(8,128)(2,1)}, u32[]{:S(2)}, u32[]{:S(2)}) async-start(bf16[32,30,16,128]{3,2,1,0:T(8,128)(2,1)} %pad_maximum_fusion), calls=%async_computation | async-start | bytes 7864320 | tf_op jit(solution)/shard_map/all_to_all | solution.py:325
  31.0 5.0 %collective-permute-start = (bf16[3,192,2048]{2,1,0:T(8,128)(2,1)}, bf16[3,192,2048]{2,1,0:T(8,128)(2,1)S(1)}, u32[]{:S(2)}, u32[]{:S(2)}) collective-permute-start(bf16[3,192,2048]{2,1,0:T(8,128)(2,1)} %expert_part.1), channel_id=1, source_target_pairs={{0,128},{128,0},{1,129},{129,1},{2,130},{130,2},{3,131},{131,3},{4... | collective-permute-start | bytes 7077896 | tf_op jit(solution)/shard_map/ppermute | solution.py:20
  39.9 5.0 %copy-start.8 = (bf16[3,96,2048]{2,1,0:T(8,128)(2,1)S(1)}, bf16[3,96,2048]{2,1,0:T(8,128)(2,1)}, u32[]{:S(2)}) copy-start(bf16[3,96,2048]{2,1,0:T(8,128)(2,1)} %layer_part.4.refs_1_) | copy-start | bytes 3538948
  39.9 27.8 %collective-permute-start.4 = (bf16[3,96,2048]{2,1,0:T(8,128)(2,1)}, bf16[3,96,2048]{2,1,0:T(8,128)(2,1)S(1)}, u32[]{:S(2)}, u32[]{:S(2)}) collective-permute-start(bf16[3,96,2048]{2,1,0:T(8,128)(2,1)} %layer_part.4.refs_1_), channel_id=1, source_target_pairs={{0,3},{1,0},{2,1},{3,2},{4,7},{5,4},{6,5},{7,6},{8,11},{9,8},{10,9... | collective-permute-start | bytes 3538952 | tf_op jit(solution)/shard_map/ppermute | solution.py:29
  44.8 28.4 %collective-permute-start.1 = (bf16[3,96,2048]{2,1,0:T(8,128)(2,1)}, bf16[3,96,2048]{2,1,0:T(8,128)(2,1)}, u32[]{:S(2)}, u32[]{:S(2)}) collective-permute-start(bf16[3,96,2048]{2,1,0:T(8,128)(2,1)} %layer_part.3.refs_0_), channel_id=1, source_target_pairs={{0,1},{1,2},{2,3},{3,0},{4,5},{5,6},{6,7},{7,4},{8,9},{9,10},{10,1... | collective-permute-start | bytes 3538952 | tf_op jit(solution)/shard_map/ppermute | solution.py:29
  44.8 75.4 %collective-permute-start.2 = (bf16[3,96,2048]{2,1,0:T(8,128)(2,1)S(1)}, bf16[3,96,2048]{2,1,0:T(8,128)(2,1)}, u32[]{:S(2)}, u32[]{:S(2)}) collective-permute-start(bf16[3,96,2048]{2,1,0:T(8,128)(2,1)S(1)} %copy-done.8), channel_id=1, source_target_pairs={{0,1},{1,2},{2,3},{3,0},{4,5},{5,6},{6,7},{7,4},{8,9},{9,10},{10,1... | collective-permute-start | bytes 3538952 | tf_op jit(solution)/shard_map/ppermute | solution.py:29
  45.1 75.1 %collective-permute-start.3 = (bf16[3,96,2048]{2,1,0:T(8,128)(2,1)}, bf16[3,96,2048]{2,1,0:T(8,128)(2,1)}, u32[]{:S(2)}, u32[]{:S(2)}) collective-permute-start(bf16[3,96,2048]{2,1,0:T(8,128)(2,1)} %layer_part.3.refs_0_), channel_id=1, source_target_pairs={{0,3},{1,0},{2,1},{3,2},{4,7},{5,4},{6,5},{7,6},{8,11},{9,8},{10,9... | collective-permute-start | bytes 3538952 | tf_op jit(solution)/shard_map/ppermute | solution.py:29
  67.7 49.8 %copy-start.13 = (bf16[3,96,2048]{2,1,0:T(8,128)(2,1)}, bf16[3,96,2048]{2,1,0:T(8,128)(2,1)S(1)}, u32[]{:S(2)}) copy-start(bf16[3,96,2048]{2,1,0:T(8,128)(2,1)S(1)} %collective-permute-done.4.refs_5_) | copy-start | bytes 3538948
  67.7 52.6 %collective-permute-start.6 = (bf16[3,96,2048]{2,1,0:T(8,128)(2,1)S(1)}, bf16[3,96,2048]{2,1,0:T(8,128)(2,1)}, u32[]{:S(2)}, u32[]{:S(2)}) collective-permute-start(bf16[3,96,2048]{2,1,0:T(8,128)(2,1)S(1)} %collective-permute-done.4.refs_5_), channel_id=1, source_target_pairs={{0,3},{1,0},{2,1},{3,2},{4,7},{5,4},{6,5},{7,6},{8,11},{9,8},{10,9... | collective-permute-start | bytes 3538952 | tf_op jit(solution)/shard_map/ppermute | solution.py:29
  73.3 50.6 %collective-permute-start.5 = (bf16[3,96,2048]{2,1,0:T(8,128)(2,1)}, bf16[3,96,2048]{2,1,0:T(8,128)(2,1)}, u32[]{:S(2)}, u32[]{:S(2)}) collective-permute-start(bf16[3,96,2048]{2,1,0:T(8,128)(2,1)} %collective-permute-done.1.refs_2_), channel_id=1, source_target_pairs={{0,1},{1,2},{2,3},{3,0},{4,5},{5,6},{6,7},{7,4},{8,9},{9,10},{10,1... | collective-permute-start | bytes 3538952 | tf_op jit(solution)/shard_map/ppermute | solution.py:29
  140.1 40.6 %all-to-all-start.1 = ((bf16[32,10,16,128]{3,2,1,0:T(8,128)(2,1)}), bf16[32,10,16,128]{3,2,1,0:T(8,128)(2,1)S(1)}, u32[]{:S(2)}, u32[]{:S(2)}) async-start(bf16[32,10,16,128]{3,2,1,0:T(8,128)(2,1)} %bitcast.39), calls=%async_computation.1 | async-start | bytes 2621440 | tf_op jit(solution)/shard_map/all_to_all | solution.py:333
  153.8 52.5 %collective-permute-start.8 = (bf16[3,192,2048]{2,1,0:T(8,128)(2,1)}, bf16[3,192,2048]{2,1,0:T(8,128)(2,1)}, u32[]{:S(2)}, u32[]{:S(2)}) collective-permute-start(bf16[3,192,2048]{2,1,0:T(8,128)(2,1)} %layer_part.5.refs_0_), channel_id=1, source_target_pairs={{0,1},{1,2},{2,3},{3,0},{4,5},{5,6},{6,7},{7,4},{8,9},{9,10},{10,1... | collective-permute-start | bytes 7077896 | tf_op jit(solution)/shard_map/ppermute | solution.py:29
  153.8 54.0 %collective-permute-start.9 = (bf16[3,192,2048]{2,1,0:T(8,128)(2,1)}, bf16[3,192,2048]{2,1,0:T(8,128)(2,1)}, u32[]{:S(2)}, u32[]{:S(2)}) collective-permute-start(bf16[3,192,2048]{2,1,0:T(8,128)(2,1)} %layer_part.5.refs_0_), channel_id=1, source_target_pairs={{0,3},{1,0},{2,1},{3,2},{4,7},{5,4},{6,5},{7,6},{8,11},{9,8},{10,9... | collective-permute-start | bytes 7077896 | tf_op jit(solution)/shard_map/ppermute | solution.py:29
  181.1 6.0 %copy-start.10 = (bf16[64,2048]{1,0:T(8,128)(2,1)S(1)}, bf16[64,2048]{1,0:T(8,128)(2,1)}, u32[]{:S(2)}) copy-start(bf16[64,2048]{1,0:T(8,128)(2,1)} %param.16) | copy-start | bytes 786436
  181.1 5.7 %collective-permute-start.7 = (f32[64,2048]{1,0:T(8,128)S(1)}, f32[64,2048]{1,0:T(8,128)S(1)}, u32[]{:S(2)}, u32[]{:S(2)}) collective-permute-start(f32[64,2048]{1,0:T(8,128)S(1)} %fusion.9), channel_id=1, source_target_pairs={{0,128},{128,0},{1,129},{129,1},{2,130},{130,2},{3,131},{131,3},{4... | collective-permute-start | bytes 1572872 | tf_op jit(solution)/shard_map/ppermute | solution.py:20
  189.2 79.8 %all-to-all-start.2 = ((bf16[32,10,16,128]{3,2,1,0:T(8,128)(2,1)}), bf16[32,10,16,128]{3,2,1,0:T(8,128)(2,1)S(1)}, u32[]{:S(2)}, u32[]{:S(2)}) async-start(bf16[32,10,16,128]{3,2,1,0:T(8,128)(2,1)} %bitcast.48), calls=%async_computation.2 | async-start | bytes 2621440 | tf_op jit(solution)/shard_map/all_to_all | solution.py:175
  207.7 26.3 %collective-permute-start.10 = (bf16[3,96,2048]{2,1,0:T(8,128)(2,1)S(1)}, bf16[3,96,2048]{2,1,0:T(8,128)(2,1)}, u32[]{:S(2)}, u32[]{:S(2)}) collective-permute-start(bf16[3,96,2048]{2,1,0:T(8,128)(2,1)S(1)} %slice.100), channel_id=1, source_target_pairs={{0,1},{1,2},{2,3},{3,0},{4,5},{5,6},{6,7},{7,4},{8,9},{9,10},{10,1... | collective-permute-start | bytes 3538952 | tf_op jit(solution)/shard_map/ppermute | solution.py:29
  210.2 25.4 %collective-permute-start.11 = (bf16[3,96,2048]{2,1,0:T(8,128)(2,1)}, bf16[3,96,2048]{2,1,0:T(8,128)(2,1)}, u32[]{:S(2)}, u32[]{:S(2)}) collective-permute-start(bf16[3,96,2048]{2,1,0:T(8,128)(2,1)} %slice.101), channel_id=1, source_target_pairs={{0,3},{1,0},{2,1},{3,2},{4,7},{5,4},{6,5},{7,6},{8,11},{9,8},{10,9... | collective-permute-start | bytes 3538952 | tf_op jit(solution)/shard_map/ppermute | solution.py:29
  216.6 49.7 %copy-start.4 = (bf16[320,2048]{1,0:T(8,128)(2,1)}, bf16[320,2048]{1,0:T(8,128)(2,1)S(1)}, u32[]{:S(2)}) copy-start(bf16[320,2048]{1,0:T(8,128)(2,1)S(1)} %broadcast_select_fusion) | copy-start | bytes 3932164
  235.6 28.8 %collective-permute-start.14 = (bf16[320,2048]{1,0:T(8,128)(2,1)S(1)}, bf16[320,2048]{1,0:T(8,128)(2,1)S(1)}, u32[]{:S(2)}, u32[]{:S(2)}) collective-permute-start(bf16[320,2048]{1,0:T(8,128)(2,1)S(1)} %broadcast_select_fusion), channel_id=1, source_target_pairs={{0,1},{1,2},{2,3},{3,0},{4,5},{5,6},{6,7},{7,4},{8,9},{9,10},{10,1... | collective-permute-start | bytes 3932168 | tf_op jit(solution)/shard_map/ppermute | solution.py:29
  235.6 29.8 %collective-permute-start.16 = (bf16[320,2048]{1,0:T(8,128)(2,1)S(1)}, bf16[320,2048]{1,0:T(8,128)(2,1)S(1)}, u32[]{:S(2)}, u32[]{:S(2)}) collective-permute-start(bf16[320,2048]{1,0:T(8,128)(2,1)S(1)} %broadcast_select_fusion), channel_id=1, source_target_pairs={{0,3},{1,0},{2,1},{3,2},{4,7},{5,4},{6,5},{7,6},{8,11},{9,8},{10,9... | collective-permute-start | bytes 3932168 | tf_op jit(solution)/shard_map/ppermute | solution.py:29
  265.4 40.9 %collective-permute-start.18 = (bf16[160,2048]{1,0:T(8,128)(2,1)}, bf16[160,2048]{1,0:T(8,128)(2,1)}, u32[]{:S(2)}, u32[]{:S(2)}) collective-permute-start(bf16[160,2048]{1,0:T(8,128)(2,1)} %slice.102), channel_id=1, source_target_pairs={{0,1},{1,2},{2,3},{3,0},{4,5},{5,6},{6,7},{7,4},{8,9},{9,10},{10,1... | collective-permute-start | bytes 1966088 | tf_op jit(solution)/shard_map/ppermute | solution.py:29
  266.3 40.0 %collective-permute-start.19 = (bf16[160,2048]{1,0:T(8,128)(2,1)}, bf16[160,2048]{1,0:T(8,128)(2,1)}, u32[]{:S(2)}, u32[]{:S(2)}) collective-permute-start(bf16[160,2048]{1,0:T(8,128)(2,1)} %slice.103), channel_id=1, source_target_pairs={{0,3},{1,0},{2,1},{3,2},{4,7},{5,4},{6,5},{7,6},{8,11},{9,8},{10,9... | collective-permute-start | bytes 1966088 | tf_op jit(solution)/shard_map/ppermute | solution.py:29
  286.7 8.6 %copy-start.11 = (bf16[4,320,384]{2,1,0:T(8,128)(2,1)S(1)}, bf16[4,320,384]{2,1,0:T(8,128)(2,1)}, u32[]{:S(2)}) copy-start(bf16[4,320,384]{2,1,0:T(8,128)(2,1)} %get-tuple-element.23) | copy-start | bytes 2949124
  286.7 33.3 %all-to-all-start.3 = ((bf16[32,10,16,128]{3,2,1,0:T(8,128)(2,1)}), bf16[32,10,16,128]{3,2,1,0:T(8,128)(2,1)}, u32[]{:S(2)}, u32[]{:S(2)}) async-start(bf16[32,10,16,128]{3,2,1,0:T(8,128)(2,1)} %bitcast.54), calls=%async_computation.3 | async-start | bytes 2621440 | tf_op jit(solution)/shard_map/all_to_all | solution.py:333
  296.8 6.3 %collective-permute-start.13 = (bf16[320,384]{1,0:T(8,128)(2,1)S(1)}, bf16[320,384]{1,0:T(8,128)(2,1)S(1)}, u32[]{:S(2)}, u32[]{:S(2)}) collective-permute-start(bf16[320,384]{1,0:T(8,128)(2,1)S(1)} %get-tuple-element.45), channel_id=1, source_target_pairs={{0,1},{1,2},{2,3},{3,0},{4,5},{5,6},{6,7},{7,4},{8,9},{9,10},{10,1... | collective-permute-start | bytes 737288 | tf_op jit(solution)/shard_map/ppermute | solution.py:29
  296.9 8.4 %collective-permute-start.15 = (bf16[320,384]{1,0:T(8,128)(2,1)S(1)}, bf16[320,384]{1,0:T(8,128)(2,1)S(1)}, u32[]{:S(2)}, u32[]{:S(2)}) collective-permute-start(bf16[320,384]{1,0:T(8,128)(2,1)S(1)} %get-tuple-element.44), channel_id=1, source_target_pairs={{0,3},{1,0},{2,1},{3,2},{4,7},{5,4},{6,5},{7,6},{8,11},{9,8},{10,9... | collective-permute-start | bytes 737288 | tf_op jit(solution)/shard_map/ppermute | solution.py:29
  299.5 7.3 %collective-permute-start.17 = (bf16[320,384]{1,0:T(8,128)(2,1)S(1)}, bf16[320,384]{1,0:T(8,128)(2,1)S(1)}, u32[]{:S(2)}, u32[]{:S(2)}) collective-permute-start(bf16[320,384]{1,0:T(8,128)(2,1)S(1)} %get-tuple-element.43), channel_id=1, source_target_pairs={{0,2},{1,3},{2,0},{3,1},{4,6},{5,7},{6,4},{7,5},{8,10},{9,11},{10,... | collective-permute-start | bytes 737288 | tf_op jit(solution)/shard_map/ppermute | solution.py:29
  309.3 23.4 %copy-start.1 = (bf16[384,2048]{1,0:T(8,128)(2,1)}, bf16[384,2048]{1,0:T(8,128)(2,1)S(1)}, u32[]{:S(2)}) copy-start(bf16[384,2048]{1,0:T(8,128)(2,1)S(1)} %add_convert_fusion.mine_ref) | copy-start | bytes 4718596
  309.3 23.4 %collective-permute-start.20 = (bf16[384,2048]{1,0:T(8,128)(2,1)S(1)}, bf16[384,2048]{1,0:T(8,128)(2,1)}, u32[]{:S(2)}, u32[]{:S(2)}) collective-permute-start(bf16[384,2048]{1,0:T(8,128)(2,1)S(1)} %add_convert_fusion.mine_ref), channel_id=1, source_target_pairs={{0,128},{128,0},{1,129},{129,1},{2,130},{130,2},{3,131},{131,3},{4... | collective-permute-start | bytes 4718600 | tf_op jit(solution)/shard_map/ppermute | solution.py:20
  321.8 16.4 %collective-permute-start.12 = (f32[64,2048]{1,0:T(8,128)S(1)}, f32[64,2048]{1,0:T(8,128)S(1)}, u32[]{:S(2)}, u32[]{:S(2)}) collective-permute-start(f32[64,2048]{1,0:T(8,128)S(1)} %fusion.6), channel_id=1, source_target_pairs={{0,128},{128,0},{1,129},{129,1},{2,130},{130,2},{3,131},{131,3},{4... | collective-permute-start | bytes 1572872 | tf_op jit(solution)/shard_map/ppermute | solution.py:20
  (7 other events, 13.2 us)
